TPU v7x, 512 devices: a whole 4x8x8 slice. The times are simulated.
512 devices in a mesh: rows: 32 (over x, z), cols: 16 (over y, core).
Axes of the slice: x: 4, y: 8, z: 8, core: 2. Of those that a mesh axis runs over, the one named last changes fastest.
Arguments:
- targets: float32 [3, 65536], P(None, 'rows'), may hold values from 0 to 1
- sources: float32 [3, 65536], P(None, 'cols'), may hold values from 0 to 1
- weights: float32 [65536], P('cols'), may hold values from 0.5 to 2
- counts: int32 [4096], P('cols'), may hold values from 8 to 16, as said below
- omega: bfloat16 [65536, 128], P('cols'), may hold values from -0.0234375 to 0.0234375
Outputs:
- basis: float32 [65536, 128], P('rows')
- projected: float32 [65536, 128], P(('cols', 'rows'))
Inputs may be any that keep to these rules, and one draw needn't show every extreme that they name: `counts`: some panel uses all 16 nodes.
All inputs are finite; a program needn't handle non-finite values.
Results may differ from a plain program's by a relative error of at most 0.0033.
Values may be sent and summed in bfloat16 or wider, within the bound.
No kernel may reach another device: no remote copies, remote signals or barrier semaphores. Data moves between devices by JAX's collectives and lax.ppermute only.
A program may use at most 64 MiB of HBM per device.

v0:
```python
import math

import jax
import jax.numpy as jnp
from jax import lax
from jax.sharding import PartitionSpec as P

wave_number = 160.0
separation = 2.0


def kernel_cols(targets, src_block, wts_block):
    diff_x = targets[0][None, :] - (src_block[0][:, None] + separation)
    diff_y = targets[1][None, :] - src_block[1][:, None]
    diff_z = targets[2][None, :] - src_block[2][:, None]
    distance = jnp.sqrt(diff_x * diff_x + diff_y * diff_y + diff_z * diff_z)
    return (wts_block[:, None] * jnp.cos(wave_number * distance) / distance).astype(jnp.bfloat16)


def contract_first(left, right):
    return lax.dot_general(
        left, right, (((0,), (0,)), ((), ())), preferred_element_type=jnp.float32
    )


def gram_of(rows_block):
    return jnp.dot(
        rows_block.T,
        rows_block,
        precision=lax.Precision.HIGHEST,
        preferred_element_type=jnp.float32,
    )


def solve_rows(rows_block, gram_matrix):
    lower_factor = jnp.linalg.cholesky(gram_matrix)
    return lax.linalg.triangular_solve(
        lower_factor, rows_block, left_side=False, lower=True, transpose_a=True
    )


def shards(targets, sources, weights, counts, omega):
    rows_here = targets.shape[1]
    cols_here = sources.shape[1]
    rank = omega.shape[1]
    panel_count = counts.shape[0]
    panel_size = cols_here // panel_count
    usable = (
        (lax.broadcasted_iota(jnp.int32, (panel_count, panel_size), 1) < counts[:, None])
        .reshape(-1)
        .astype(jnp.float32)
    )
    node_weight = weights * usable
    block_width = math.gcd(cols_here, 512)
    nblocks = cols_here // block_width
    src_blocks = sources.reshape(3, nblocks, block_width).transpose(1, 0, 2)
    wts_blocks = node_weight.reshape(nblocks, block_width)
    omega_blocks = omega.reshape(nblocks, block_width, rank)

    def sketch_turn(total, inputs):
        kernel_tile = kernel_cols(targets, inputs[0], inputs[1])
        return (total + contract_first(kernel_tile, inputs[2]), None)

    partial_sketch, _ = lax.scan(
        sketch_turn,
        jnp.zeros((rows_here, rank), jnp.float32),
        (src_blocks, wts_blocks, omega_blocks),
    )
    sketch = lax.psum(partial_sketch, "cols")
    gram_matrix = lax.psum(gram_of(sketch), "rows")
    ortho = solve_rows(sketch, gram_matrix)
    ortho_low = ortho.astype(jnp.bfloat16)
    row_devices = lax.axis_size("rows")
    own_count = cols_here // row_devices
    inner_width = math.gcd(lax.axis_size("rows") * own_count, 512)
    inner_blocks = lax.axis_size("rows") * own_count // inner_width
    sub_src_blocks = sources.reshape(3, inner_blocks, inner_width).transpose(1, 0, 2)
    sub_wts_blocks = node_weight.reshape(inner_blocks, inner_width)

    def project_block(inputs):
        kernel_tile = kernel_cols(targets, inputs[0], inputs[1])
        return jnp.dot(kernel_tile, ortho_low, preferred_element_type=jnp.float32)

    projected = lax.psum_scatter(
        lax.map(project_block, (sub_src_blocks, sub_wts_blocks)).reshape(
            lax.axis_size("rows") * own_count, rank
        ),
        "rows",
        scatter_dimension=0,
        tiled=True,
    )
    scaled = ortho * math.sqrt(rows_here * row_devices)
    return (scaled, projected)


def solution(mesh):
    return jax.shard_map(
        shards,
        mesh=mesh,
        in_specs=(P(None, "rows"), P(None, "cols"), P("cols"), P("cols"), P("cols", None)),
        out_specs=(P("rows", None), P(("cols", "rows"), None)),
        check_vma=False,
    )
```

profile of v0, /device:TPU:1, one launch (start us, length us, event | category | flops | bytes accessed | tf_op | source)
XLA Modules:
  0.0 841.0 jit_solution(1076110894502836828)
XLA Ops:
  7.2 0.0 all-reduce.3.cloned.1.call-start
  7.2 0.8 iota_compare_fusion
  8.0 0.1 lt.20
  8.1 0.7 broadcast_select_fusion
  8.9 154.4 %while.22 = (s32[]{:T(128)}, f32[2048,128]{1,0:T(8,128)S(1)}, f32[8,512]{1,0:T(8,128)S(1)}, f32[3,2048]{1,0:T(4,128)}, f32[8,3,512]{2,1,0:T(4,128)}, /*index=5*/...) while((s32[]{:T(128)}, f32[2048,128]{1,0:T(8,128)S(1)}, f32[8,512]{1,0:T(8,128)S(1)}, ...), condition=%wide.region_1.2_spmd.clone, body=%wide.region_0.1_spmd.clone.sunk | while | flops 281543168 | bytes 2327191 | solution.py:64
  8.9 0.8 dynamic-slice_add_fusion.5
  9.7 0.9 fusion.36
  10.6 17.5 %convolution_add_fusion.2 = f32[2048,128]{1,0:T(8,128)S(1)} fusion(f32[512]{0:T(512)S(1)} %bitcast.85, f32[2048]{0:T(1024)S(1)} %bitcast.77, f32[512]{0:T(512)S(1)} %bitcast.84, f32[2048]{0:T(1024)S(1)} %bitcast.78, f32[512]{0:T(512)S(1)} %bitcast.83, f32[2048]{0:T(1024)S(1)} %bitcast.76, f32[512]{0:T(512)S(1)} %bitcast.89, ...), kind=kOutput, calls=%fused_computation.10.clone.1 | convolution fusion | flops 281542656 | bytes 2261505 | tf_op jit(solution)/shard_map/while/body/eval_jaxpr/dot_general | solution.py:21
  28.1 0.8 dynamic-slice_add_fusion.5
  29.0 0.9 fusion.36
  29.9 17.5 %convolution_add_fusion.2 = f32[2048,128]{1,0:T(8,128)S(1)} fusion(f32[512]{0:T(512)S(1)} %bitcast.85, f32[2048]{0:T(1024)S(1)} %bitcast.77, f32[512]{0:T(512)S(1)} %bitcast.84, f32[2048]{0:T(1024)S(1)} %bitcast.78, f32[512]{0:T(512)S(1)} %bitcast.83, f32[2048]{0:T(1024)S(1)} %bitcast.76, f32[512]{0:T(512)S(1)} %bitcast.89, ...), kind=kOutput, calls=%fused_computation.10.clone.1 | convolution fusion | flops 281542656 | bytes 2261505 | tf_op jit(solution)/shard_map/while/body/eval_jaxpr/dot_general | solution.py:21
  47.4 0.8 dynamic-slice_add_fusion.5
  48.2 0.9 fusion.36
  49.1 17.5 %convolution_add_fusion.2 = f32[2048,128]{1,0:T(8,128)S(1)} fusion(f32[512]{0:T(512)S(1)} %bitcast.85, f32[2048]{0:T(1024)S(1)} %bitcast.77, f32[512]{0:T(512)S(1)} %bitcast.84, f32[2048]{0:T(1024)S(1)} %bitcast.78, f32[512]{0:T(512)S(1)} %bitcast.83, f32[2048]{0:T(1024)S(1)} %bitcast.76, f32[512]{0:T(512)S(1)} %bitcast.89, ...), kind=kOutput, calls=%fused_computation.10.clone.1 | convolution fusion | flops 281542656 | bytes 2261505 | tf_op jit(solution)/shard_map/while/body/eval_jaxpr/dot_general | solution.py:21
  66.7 0.8 dynamic-slice_add_fusion.5
  67.5 0.9 fusion.36
  68.4 17.5 %convolution_add_fusion.2 = f32[2048,128]{1,0:T(8,128)S(1)} fusion(f32[512]{0:T(512)S(1)} %bitcast.85, f32[2048]{0:T(1024)S(1)} %bitcast.77, f32[512]{0:T(512)S(1)} %bitcast.84, f32[2048]{0:T(1024)S(1)} %bitcast.78, f32[512]{0:T(512)S(1)} %bitcast.83, f32[2048]{0:T(1024)S(1)} %bitcast.76, f32[512]{0:T(512)S(1)} %bitcast.89, ...), kind=kOutput, calls=%fused_computation.10.clone.1 | convolution fusion | flops 281542656 | bytes 2261505 | tf_op jit(solution)/shard_map/while/body/eval_jaxpr/dot_general | solution.py:21
  86.0 0.8 dynamic-slice_add_fusion.5
  86.8 0.9 fusion.36
  87.7 17.5 %convolution_add_fusion.2 = f32[2048,128]{1,0:T(8,128)S(1)} fusion(f32[512]{0:T(512)S(1)} %bitcast.85, f32[2048]{0:T(1024)S(1)} %bitcast.77, f32[512]{0:T(512)S(1)} %bitcast.84, f32[2048]{0:T(1024)S(1)} %bitcast.78, f32[512]{0:T(512)S(1)} %bitcast.83, f32[2048]{0:T(1024)S(1)} %bitcast.76, f32[512]{0:T(512)S(1)} %bitcast.89, ...), kind=kOutput, calls=%fused_computation.10.clone.1 | convolution fusion | flops 281542656 | bytes 2261505 | tf_op jit(solution)/shard_map/while/body/eval_jaxpr/dot_general | solution.py:21
  105.2 0.8 dynamic-slice_add_fusion.5
  106.1 0.9 fusion.36
  107.0 17.5 %convolution_add_fusion.2 = f32[2048,128]{1,0:T(8,128)S(1)} fusion(f32[512]{0:T(512)S(1)} %bitcast.85, f32[2048]{0:T(1024)S(1)} %bitcast.77, f32[512]{0:T(512)S(1)} %bitcast.84, f32[2048]{0:T(1024)S(1)} %bitcast.78, f32[512]{0:T(512)S(1)} %bitcast.83, f32[2048]{0:T(1024)S(1)} %bitcast.76, f32[512]{0:T(512)S(1)} %bitcast.89, ...), kind=kOutput, calls=%fused_computation.10.clone.1 | convolution fusion | flops 281542656 | bytes 2261505 | tf_op jit(solution)/shard_map/while/body/eval_jaxpr/dot_general | solution.py:21
  124.5 0.8 dynamic-slice_add_fusion.5
  125.4 0.9 fusion.36
  126.3 17.5 %convolution_add_fusion.2 = f32[2048,128]{1,0:T(8,128)S(1)} fusion(f32[512]{0:T(512)S(1)} %bitcast.85, f32[2048]{0:T(1024)S(1)} %bitcast.77, f32[512]{0:T(512)S(1)} %bitcast.84, f32[2048]{0:T(1024)S(1)} %bitcast.78, f32[512]{0:T(512)S(1)} %bitcast.83, f32[2048]{0:T(1024)S(1)} %bitcast.76, f32[512]{0:T(512)S(1)} %bitcast.89, ...), kind=kOutput, calls=%fused_computation.10.clone.1 | convolution fusion | flops 281542656 | bytes 2261505 | tf_op jit(solution)/shard_map/while/body/eval_jaxpr/dot_general | solution.py:21
  143.8 0.8 dynamic-slice_add_fusion.5
  144.6 0.9 fusion.36
  145.5 17.5 %convolution_add_fusion.2 = f32[2048,128]{1,0:T(8,128)S(1)} fusion(f32[512]{0:T(512)S(1)} %bitcast.85, f32[2048]{0:T(1024)S(1)} %bitcast.77, f32[512]{0:T(512)S(1)} %bitcast.84, f32[2048]{0:T(1024)S(1)} %bitcast.78, f32[512]{0:T(512)S(1)} %bitcast.83, f32[2048]{0:T(1024)S(1)} %bitcast.76, f32[512]{0:T(512)S(1)} %bitcast.89, ...), kind=kOutput, calls=%fused_computation.10.clone.1 | convolution fusion | flops 281542656 | bytes 2261505 | tf_op jit(solution)/shard_map/while/body/eval_jaxpr/dot_general | solution.py:21
  163.3 0.0 copy-start.2
  163.3 1.0 copy-done.2
  164.2 0.0 all-reduce.3.cloned.1.call-update
  164.3 0.0 all-reduce.5.cloned.1.call-start
  164.3 122.9 %all-reduce.3.cloned.1.call-done = f32[2048,128]{1,0:T(8,128)} async-done(((f32[2048,128]{1,0:T(8,128)}), f32[2048,128]{1,0:T(8,128)}) %all-reduce.3.cloned.1.call-update) | async-done | bytes 1048592 | tf_op jit(solution)/shard_map/psum | solution.py:69
  287.2 4.1 fusion.22
  291.3 0.0 all-reduce.5.cloned.1.call-update
  291.3 0.0 reduce-scatter.2.cloned.1.call-start
  291.4 149.7 %all-reduce.5.cloned.1.call-done = f32[128,128]{0,1:T(8,128)} async-done(((f32[128,128]{0,1:T(8,128)}), f32[128,128]{0,1:T(8,128)}) %all-reduce.5.cloned.1.call-update) | async-done | bytes 65552 | tf_op jit(solution)/shard_map/psum | solution.py:70
  441.0 0.9 copy.10
  442.0 0.9 fusion.18
  442.8 11.7 %cholesky.16 = f32[128,128]{1,0:T(8,128)S(1)} custom-call(f32[128,128]{1,0:T(8,128)S(1)} %fusion.18), custom_call_target="Cholesky" | custom-call | tf_op jit(solution)/shard_map/jit(cholesky)/cholesky | solution.py:36
  454.6 0.6 compare_reduce_fusion
  455.2 0.7 fusion.15
  455.9 9.8 %custom-call.6 = f32[1,128,128]{1,2,0:T(8,128)S(1)} custom-call(f32[1,128,128]{2,1,0:T(8,128)S(1)} %fusion.15), custom_call_target="InvertDiagBlocksLowerTriangular" | custom-call | tf_op jit(solution)/shard_map/triangular_solve | solution.py:37
  465.7 1.9 fusion.21
  467.7 144.9 %while.21 = (s32[]{:T(128)}, f32[8,512,128]{2,1,0:T(8,128)}, f32[8,512]{1,0:T(8,128)S(1)}, f32[3,2048]{1,0:T(4,128)S(1)}, f32[8,3,512]{2,1,0:T(4,128)}, /*index=...) while((s32[]{:T(128)}, f32[8,512,128]{2,1,0:T(8,128)}, f32[8,512]{1,0:T(8,128)S(1)}, ...), condition=%wide.region_7.8_spmd, body=%wide.region_6.7_spmd.sunk | while | flops 281018880 | bytes 885389 | solution.py:85
  467.7 0.8 dynamic-slice_add_fusion.4
  468.5 17.3 %fusion.34 = f32[8,512,128]{2,1,0:T(8,128)} fusion(f32[8,512,128]{2,1,0:T(8,128)} %get-tuple-element.266, s32[]{:T(128)} %get-tuple-element.265, bf16[2048,128]{1,0:T(8,128)(2,1)S(1)} %get-tuple-element.280, f32[512]{0:T(512)S(1)} %bitcast.88, f32[2048]{0:T(1024)S(1)} %bitcast.80, f32[512]{0:T(512)S(1)} %bitcast.87, f32[2048]{0:T(1024)S(1)} %bitcast.81, ...), kind=kOutput, calls=%fused_computation.3.clone.1 | convolution fusion | flops 281018368 | bytes 819712 | tf_op jit(solution)/shard_map/while/body/eval_jaxpr/dot_general | solution.py:82
  485.8 0.8 dynamic-slice_add_fusion.4
  486.6 17.3 %fusion.34 = f32[8,512,128]{2,1,0:T(8,128)} fusion(f32[8,512,128]{2,1,0:T(8,128)} %get-tuple-element.266, s32[]{:T(128)} %get-tuple-element.265, bf16[2048,128]{1,0:T(8,128)(2,1)S(1)} %get-tuple-element.280, f32[512]{0:T(512)S(1)} %bitcast.88, f32[2048]{0:T(1024)S(1)} %bitcast.80, f32[512]{0:T(512)S(1)} %bitcast.87, f32[2048]{0:T(1024)S(1)} %bitcast.81, ...), kind=kOutput, calls=%fused_computation.3.clone.1 | convolution fusion | flops 281018368 | bytes 819712 | tf_op jit(solution)/shard_map/while/body/eval_jaxpr/dot_general | solution.py:82
  503.9 0.8 dynamic-slice_add_fusion.4
  504.7 17.3 %fusion.34 = f32[8,512,128]{2,1,0:T(8,128)} fusion(f32[8,512,128]{2,1,0:T(8,128)} %get-tuple-element.266, s32[]{:T(128)} %get-tuple-element.265, bf16[2048,128]{1,0:T(8,128)(2,1)S(1)} %get-tuple-element.280, f32[512]{0:T(512)S(1)} %bitcast.88, f32[2048]{0:T(1024)S(1)} %bitcast.80, f32[512]{0:T(512)S(1)} %bitcast.87, f32[2048]{0:T(1024)S(1)} %bitcast.81, ...), kind=kOutput, calls=%fused_computation.3.clone.1 | convolution fusion | flops 281018368 | bytes 819712 | tf_op jit(solution)/shard_map/while/body/eval_jaxpr/dot_general | solution.py:82
  522.0 0.8 dynamic-slice_add_fusion.4
  522.8 17.3 %fusion.34 = f32[8,512,128]{2,1,0:T(8,128)} fusion(f32[8,512,128]{2,1,0:T(8,128)} %get-tuple-element.266, s32[]{:T(128)} %get-tuple-element.265, bf16[2048,128]{1,0:T(8,128)(2,1)S(1)} %get-tuple-element.280, f32[512]{0:T(512)S(1)} %bitcast.88, f32[2048]{0:T(1024)S(1)} %bitcast.80, f32[512]{0:T(512)S(1)} %bitcast.87, f32[2048]{0:T(1024)S(1)} %bitcast.81, ...), kind=kOutput, calls=%fused_computation.3.clone.1 | convolution fusion | flops 281018368 | bytes 819712 | tf_op jit(solution)/shard_map/while/body/eval_jaxpr/dot_general | solution.py:82
  540.1 0.8 dynamic-slice_add_fusion.4
  541.0 17.2 %fusion.34 = f32[8,512,128]{2,1,0:T(8,128)} fusion(f32[8,512,128]{2,1,0:T(8,128)} %get-tuple-element.266, s32[]{:T(128)} %get-tuple-element.265, bf16[2048,128]{1,0:T(8,128)(2,1)S(1)} %get-tuple-element.280, f32[512]{0:T(512)S(1)} %bitcast.88, f32[2048]{0:T(1024)S(1)} %bitcast.80, f32[512]{0:T(512)S(1)} %bitcast.87, f32[2048]{0:T(1024)S(1)} %bitcast.81, ...), kind=kOutput, calls=%fused_computation.3.clone.1 | convolution fusion | flops 281018368 | bytes 819712 | tf_op jit(solution)/shard_map/while/body/eval_jaxpr/dot_general | solution.py:82
  558.2 0.8 dynamic-slice_add_fusion.4
  559.1 17.2 %fusion.34 = f32[8,512,128]{2,1,0:T(8,128)} fusion(f32[8,512,128]{2,1,0:T(8,128)} %get-tuple-element.266, s32[]{:T(128)} %get-tuple-element.265, bf16[2048,128]{1,0:T(8,128)(2,1)S(1)} %get-tuple-element.280, f32[512]{0:T(512)S(1)} %bitcast.88, f32[2048]{0:T(1024)S(1)} %bitcast.80, f32[512]{0:T(512)S(1)} %bitcast.87, f32[2048]{0:T(1024)S(1)} %bitcast.81, ...), kind=kOutput, calls=%fused_computation.3.clone.1 | convolution fusion | flops 281018368 | bytes 819712 | tf_op jit(solution)/shard_map/while/body/eval_jaxpr/dot_general | solution.py:82
  576.3 0.8 dynamic-slice_add_fusion.4
  577.2 17.2 %fusion.34 = f32[8,512,128]{2,1,0:T(8,128)} fusion(f32[8,512,128]{2,1,0:T(8,128)} %get-tuple-element.266, s32[]{:T(128)} %get-tuple-element.265, bf16[2048,128]{1,0:T(8,128)(2,1)S(1)} %get-tuple-element.280, f32[512]{0:T(512)S(1)} %bitcast.88, f32[2048]{0:T(1024)S(1)} %bitcast.80, f32[512]{0:T(512)S(1)} %bitcast.87, f32[2048]{0:T(1024)S(1)} %bitcast.81, ...), kind=kOutput, calls=%fused_computation.3.clone.1 | convolution fusion | flops 281018368 | bytes 819712 | tf_op jit(solution)/shard_map/while/body/eval_jaxpr/dot_general | solution.py:82
  594.4 0.8 dynamic-slice_add_fusion.4
  595.3 17.3 %fusion.34 = f32[8,512,128]{2,1,0:T(8,128)} fusion(f32[8,512,128]{2,1,0:T(8,128)} %get-tuple-element.266, s32[]{:T(128)} %get-tuple-element.265, bf16[2048,128]{1,0:T(8,128)(2,1)S(1)} %get-tuple-element.280, f32[512]{0:T(512)S(1)} %bitcast.88, f32[2048]{0:T(1024)S(1)} %bitcast.80, f32[512]{0:T(512)S(1)} %bitcast.87, f32[2048]{0:T(1024)S(1)} %bitcast.81, ...), kind=kOutput, calls=%fused_computation.3.clone.1 | convolution fusion | flops 281018368 | bytes 819712 | tf_op jit(solution)/shard_map/while/body/eval_jaxpr/dot_general | solution.py:82
  612.5 0.0 reduce-scatter.2.cloned.1.call-update
  612.5 221.9 %reduce-scatter.2.cloned.1.call-done = f32[128,128]{1,0:T(8,128)} async-done(((f32[4096,128]{1,0:T(8,128)}), f32[128,128]{1,0:T(8,128)}) %reduce-scatter.2.cloned.1.call-update) | async-done | bytes 65552 | tf_op jit(solution)/shard_map/reduce_scatter | solution.py:84
  (32 shorter events, 0.3 us)
Async XLA Ops:
  7.2 280.0 %all-reduce.3.cloned.1.call-start = ((), (), s32[]{:S(2)}) async-start(), calls=%async_computation.1 | async-start | bytes 2097152 | tf_op jit(solution)/shard_map/psum | solution.py:69
  163.3 1.0 copy-start.2
  164.3 276.8 %all-reduce.5.cloned.1.call-start = ((), (), s32[]{:S(2)}) async-start(), calls=%async_computation.2 | async-start | bytes 131072 | tf_op jit(solution)/shard_map/psum | solution.py:70
  287.2 178.5 %copy-start = (f32[2048,128]{1,0:T(8,128)S(1)}, f32[2048,128]{1,0:T(8,128)}, u32[]{:S(2)}) copy-start(f32[2048,128]{1,0:T(8,128)} %all-reduce.3.cloned.1.call-done) | copy-start | bytes 3145732
  291.3 176.4 %copy-start.1 = (f32[3,2048]{1,0:T(4,128)S(1)}, f32[3,2048]{1,0:T(4,128)}, u32[]{:S(2)}) copy-start(f32[3,2048]{1,0:T(4,128)} %get-tuple-element.291) | copy-start | bytes 73732
  291.3 543.1 %reduce-scatter.2.cloned.1.call-start = ((), (), s32[]{:S(2)}) async-start(), calls=%async_computation.3 | async-start | bytes 2162688 | tf_op jit(solution)/shard_map/reduce_scatter | solution.py:84
Sparse Core Ops, SparseCore 0:
  164.4 122.7 all-reduce.2
  291.4 149.5 all-reduce.4
  612.7 221.7 reduce-scatter.1
where the time goes:
time: 847 us; the launch traced here: 841 us
  waiting for transfers between devices  495 us (58%)
  matrix products  284 us (34%)
  other arithmetic  38.3 us (5%)
  between operations  13.8 us (2%)
  local copies, waits for them, and re-layouts  9.44 us (1%)
    reduce_scatter x1, waiting for transfers between devices, shards(): lax.psum_scatter(lax.map(project_block, (sub_src_blocks, sub_wts_blocks))...  222 us
    psum x1, waiting for transfers between devices, shards(): gram_matrix = lax.psum(gram_of(sketch), 'rows')  150 us
    dot_general x8, matrix products, contract_first(): lax.dot_general(left, right, (((0,), (0,)), ((), ())), preferred_element_...  140 us
    dot_general x8, matrix products, project_block(): return jnp.dot(kernel_tile, ortho_low, preferred_element_type=jnp.float32)  138 us
    psum x1, waiting for transfers between devices, shards(): sketch = lax.psum(partial_sketch, 'cols')  123 us
  transfers between devices with their start and end apart: 3, of which 3 were waited for; matrix products, arithmetic and copies ran while one was open for 0% of the time, Pallas kernels for 0%

commit v1 on v0

v1 whole, which is shorter than its diff:
```python
import functools
import math

import jax
import jax.numpy as jnp
from jax import lax
from jax.experimental import pallas as pl
from jax.experimental.pallas import tpu as pltpu
from jax.sharding import PartitionSpec as P

f32 = jnp.float32
bf16 = jnp.bfloat16
wave_number = 160.0
separation = 2.0
turns = wave_number / (2.0 * math.pi)
sine = (6.283164043875678, -41.33714231633244, 81.34076713243772, -70.99341720807224)
target_tile = 256
source_tile = 512


def thirds(values):
    high = values.astype(bf16)
    rest = values - high.astype(f32)
    middle = rest.astype(bf16)
    low = (rest - middle.astype(f32)).astype(bf16)
    return high, middle, low


def pick_rows(rows, shape):
    at = lax.broadcasted_iota(jnp.int32, shape, 0)
    out = jnp.zeros(shape, f32)
    for k, row in enumerate(rows):
        out = jnp.where(at == k, jnp.broadcast_to(row, shape), out)
    return out


def put_thirds(ref, values, outer):
    parts = [part.astype(f32) for part in thirds(values)]
    for p in range(3):
        for q in range(3):
            k = 3 * p + q
            ref[8 * k : 8 * k + 8, :] = parts[p if outer else q]


def sketch_kernel(targets, sources, weights, usable, omega, tiles, sketch,
                  feature, tfeat, afeat, bfeat, masked, a_buf, b_buf, acc):
    step = pl.program_id(0)
    ncols = sources.shape[1]
    turns_n = ncols // source_tile

    @pl.when(step == 0)
    def _():
        nrows = targets.shape[1]
        feature[...] = jnp.zeros_like(feature)
        tx = (targets[0:1, :] - (0.5 + 0.5 * separation)) * turns
        ty = (targets[1:2, :] - 0.5) * turns
        tz = (targets[2:3, :] - 0.5) * turns
        rows = [tx, ty, tz, tx * tx + ty * ty + tz * tz, jnp.ones_like(tx)]
        view = feature.at[:, 0:nrows]
        put_thirds(view, pick_rows(rows, (8, nrows)), True)
        for k in range(nrows // 128):
            tfeat[128 * k : 128 * k + 128, :] = feature[:, 128 * k : 128 * k + 128].T.astype(bf16)
        sx = (sources[0:1, :] + (0.5 * separation - 0.5)) * turns
        sy = (sources[1:2, :] - 0.5) * turns
        sz = (sources[2:3, :] - 0.5) * turns
        norm = sx * sx + sy * sy + sz * sz
        inverse = 1.0 / weights[...]
        for ref, scale in ((bfeat, inverse), (afeat, inverse * inverse)):
            rows = [-2.0 * sx * scale, -2.0 * sy * scale, -2.0 * sz * scale, scale, norm * scale]
            put_thirds(feature, pick_rows(rows, (8, ncols)), False)
            ref[...] = feature[...].astype(bf16)
        flag = pick_rows([usable[...]], (8, ncols)).astype(bf16)
        column = lax.dot_general(
            flag, jnp.ones((8, omega.shape[1]), bf16), (((0,), (0,)), ((), ())), preferred_element_type=f32
        )
        masked[...] = (omega[...].astype(f32) * column).astype(bf16)

    here = tfeat[pl.ds(pl.multiple_of(step * target_tile, target_tile), target_tile), :]

    def cols(j):
        return pl.ds(pl.multiple_of(j * source_tile, source_tile), source_tile)

    def distances(j):
        slot = lax.rem(j, 2)
        a_buf[slot] = jnp.dot(here, afeat[:, cols(j)], preferred_element_type=f32)
        b_buf[slot] = jnp.dot(here, bfeat[:, cols(j)], preferred_element_type=f32)

    def evaluate(j):
        slot = lax.rem(j, 2)
        for r in range(0, target_tile, 16):
            a = a_buf[slot, r : r + 16, :]
            b = b_buf[slot, r : r + 16, :]
            over = lax.rsqrt(a)
            turn = b * over
            away = 0.25 - jnp.abs(turn - jnp.round(turn))
            square = away * away
            c0, c1, c2, c3 = (turns * c for c in sine)
            wave = ((c3 * square + c2) * square + c1) * square + c0
            tiles[r : r + 16, cols(j)] = ((wave * away) * over).astype(bf16)

    def accumulate(j):
        acc[...] += jnp.dot(tiles[:, cols(j)], masked[cols(j), :], preferred_element_type=f32)

    acc[...] = jnp.zeros_like(acc)
    distances(0)
    distances(1)
    evaluate(0)

    def turn(j, carry):
        distances(lax.rem(j + 1, turns_n))
        evaluate(j)
        accumulate(j - 1)
        return carry

    lax.fori_loop(1, turns_n, turn, 0)
    accumulate(turns_n - 1)
    sketch[...] = acc[...].astype(bf16)


def make_sketch(targets, sources, weights, usable, omega):
    nrows, ncols, rank = targets.shape[1], sources.shape[1], omega.shape[1]
    whole = lambda i: (0, 0)
    once = dict(pipeline_mode=pl.Buffered(1))
    return pl.pallas_call(
        sketch_kernel,
        grid=(nrows // target_tile,),
        in_specs=[
            pl.BlockSpec((3, nrows), whole, **once),
            pl.BlockSpec((3, ncols), whole, **once),
            pl.BlockSpec((1, ncols), whole, **once),
            pl.BlockSpec((1, ncols), whole, **once),
            pl.BlockSpec((ncols, rank), whole, **once),
        ],
        out_specs=[
            pl.BlockSpec((target_tile, ncols), lambda i: (i, 0)),
            pl.BlockSpec((target_tile, rank), lambda i: (i, 0)),
        ],
        out_shape=[
            jax.ShapeDtypeStruct((nrows, ncols), bf16),
            jax.ShapeDtypeStruct((nrows, rank), bf16),
        ],
        scratch_shapes=[
            pltpu.VMEM((128, ncols), f32),
            pltpu.VMEM((nrows, 128), bf16),
            pltpu.VMEM((128, ncols), bf16),
            pltpu.VMEM((128, ncols), bf16),
            pltpu.VMEM((ncols, rank), bf16),
            pltpu.VMEM((2, target_tile, source_tile), f32),
            pltpu.VMEM((2, target_tile, source_tile), f32),
            pltpu.VMEM((target_tile, rank), f32),
        ],
        name="sketch",
    )(targets, sources, weights, usable, omega)


def piece_kernel(parts, out):
    total = parts[0].astype(f32)
    for k in range(1, parts.shape[0]):
        total += parts[k].astype(f32)
    low = total.astype(bf16)
    for k in range(out.shape[0]):
        out[k] = low


def add_pieces(parts):
    return pl.pallas_call(
        piece_kernel, out_shape=jax.ShapeDtypeStruct(parts.shape, bf16), name="pieces"
    )(parts)


def project_kernel(sketch, tiles, usable, out, flipped, gram):
    rank = sketch.shape[1]
    band = gram.shape[0] // lax.axis_size("cols")

    @pl.when(pl.program_id(0) == 0)
    def _():
        flipped[...] = sketch[...].astype(f32).T.astype(bf16)
        gram[...] = jnp.dot(flipped[...], sketch[...], preferred_element_type=f32)

    product = jnp.dot(flipped[...], tiles[...], preferred_element_type=f32)
    product = (product * usable[...]).astype(bf16)
    first = pl.multiple_of(lax.axis_index("cols") * band, band)
    own = jnp.concatenate([part.astype(f32) for part in thirds(gram[pl.ds(first, band), :])], axis=0)
    own = jnp.concatenate([own, jnp.zeros((32 - 3 * band, rank), f32)], axis=0).astype(bf16)
    for k in range(out.shape[0]):
        out[k, 0:rank, :] = product[:, 128 * k : 128 * k + 128]
        out[k, rank : rank + 32, :] = own


def project(sketch, tiles, usable, row_devices):
    nrows, ncols = tiles.shape
    rank = sketch.shape[1]
    width = 512
    dests = width // (ncols // row_devices)
    return pl.pallas_call(
        project_kernel,
        grid=(ncols // width,),
        in_specs=[
            pl.BlockSpec((nrows, rank), lambda j: (0, 0), pipeline_mode=pl.Buffered(1)),
            pl.BlockSpec((nrows, width), lambda j: (0, j)),
            pl.BlockSpec((1, width), lambda j: (0, j)),
        ],
        out_specs=pl.BlockSpec((dests, rank + 32, 128), lambda j: (j, 0, 0)),
        out_shape=jax.ShapeDtypeStruct((row_devices, rank + 32, 128), bf16),
        scratch_shapes=[pltpu.VMEM((rank, nrows), bf16), pltpu.VMEM((rank, rank), f32)],
        name="project",
    )(sketch, tiles, usable)


def fold_kernel(parts, product, band):
    total = parts[0].astype(f32)
    for k in range(1, parts.shape[0]):
        total += parts[k].astype(f32)
    rank = product.shape[0]
    rows = band.shape[1]
    product[...] = total[0:rank]
    own = total[rank : rank + rows] + (
        total[rank + rows : rank + 2 * rows] + total[rank + 2 * rows : rank + 3 * rows]
    )
    for k in range(band.shape[0]):
        band[k] = own


def fold(parts, col_devices):
    rank = parts.shape[1] - 32
    return pl.pallas_call(
        fold_kernel,
        out_shape=[
            jax.ShapeDtypeStruct((rank, rank), f32),
            jax.ShapeDtypeStruct((col_devices, rank // col_devices, rank), f32),
        ],
        name="fold",
    )(parts)


def finish_kernel(scale, sketch, product, inverse, basis, projected):
    high, middle, low = thirds(inverse[...] * scale)
    contract = (((1,), (1,)), ((), ()))
    rows = sketch[...]
    total = lax.dot_general(rows, low, contract, preferred_element_type=f32)
    total += lax.dot_general(rows, middle, contract, preferred_element_type=f32)
    basis[...] = total + lax.dot_general(rows, high, contract, preferred_element_type=f32)
    projected[...] = lax.dot_general(
        product[...].T,
        inverse[...],
        contract,
        precision=lax.Precision.HIGHEST,
        preferred_element_type=f32,
    )


def finish(sketch, product, inverse, scale):
    return pl.pallas_call(
        functools.partial(finish_kernel, scale),
        out_shape=[
            jax.ShapeDtypeStruct(sketch.shape, f32),
            jax.ShapeDtypeStruct(product.shape, f32),
        ],
        name="finish",
    )(sketch, product, inverse)


def shards(targets, sources, weights, counts, omega):
    rows_here, cols_here, rank = targets.shape[1], sources.shape[1], omega.shape[1]
    row_devices, col_devices = lax.axis_size("rows"), lax.axis_size("cols")
    panel_count = counts.shape[0]
    usable = (
        (lax.broadcasted_iota(jnp.int32, (panel_count, cols_here // panel_count), 1) < counts[:, None])
        .reshape(1, cols_here)
        .astype(f32)
    )
    tiles, partial = make_sketch(targets, sources, weights.reshape(1, cols_here), usable, omega)
    pieces = lax.all_to_all(partial.reshape(col_devices, -1, rank), "cols", 0, 0)
    sketch = lax.all_to_all(add_pieces(pieces), "cols", 0, 0).reshape(rows_here, rank)
    terms = lax.all_to_all(project(sketch, tiles, usable, row_devices), "rows", 0, 0)
    product, band = fold(terms, col_devices)
    gram_matrix = lax.all_to_all(band, "cols", 0, 0).reshape(rank, rank)
    lower_factor = jnp.linalg.cholesky(gram_matrix)
    inverse = lax.linalg.triangular_solve(lower_factor, jnp.eye(rank, dtype=f32), left_side=True, lower=True)
    return finish(sketch, product, inverse, math.sqrt(rows_here * row_devices))


def solution(mesh):
    return jax.shard_map(
        shards,
        mesh=mesh,
        in_specs=(P(None, "rows"), P(None, "cols"), P("cols"), P("cols"), P("cols", None)),
        out_specs=(P("rows", None), P(("cols", "rows"), None)),
        check_vma=False,
    )
```

time: 847 us -> 207 us (0.24)
  waiting for transfers between devices: 495 us -> 0 us
  matrix products: 284 us -> 0.87 us
  blocking collectives: 0 us -> 105 us
  Pallas kernels: 0 us -> 75.6 us
  other arithmetic: 38.3 us -> 23.6 us
  between operations: 13.8 us -> 0.67 us
  local copies, waits for them, and re-layouts: 9.44 us -> 0.8 us
    dot_general x17 -> x0, matrix products: 282 us -> none  [the longest x8 140 us: contract_first(): lax.dot_general(left, right, (((0,), (0,)), ((), ())), preferred_element_...]
    psum x2 -> x0, waiting for transfers between devices: 273 us -> none  [the longest x1 150 us: shards(): gram_matrix = lax.psum(gram_of(sketch), 'rows')]
    reduce_scatter x1 -> x0, waiting for transfers between devices: 222 us -> none  [shards(): lax.psum_scatter(lax.map(project_block, (sub_src_blocks, sub_wts_blocks))...]
    all_to_all x0 -> x4, blocking collectives: none -> 105 us  [the longest x1 44.6 us: shards(): lax.all_to_all(project(sketch, tiles, usable, row_devices), 'rows', 0, 0)]
    pallas_call x0 -> x5, Pallas kernels: none -> 75.6 us  [the longest x1 57.4 us: make_sketch(): pl.pallas_call(sketch_kernel, grid=(nrows // target_tile,), in_specs=[pl....]
    add x16 -> x0, other arithmetic: 13.1 us -> none  [kernel_cols(): diff_x = targets[0][None, :] - (src_block[0][:, None] + separation)]
  transfers between devices with their start and end apart: 3 -> 0, of which waited for: 3 -> 0; matrix products, arithmetic and copies ran while one was open for 0% -> 0% of each run, Pallas kernels for 0% -> 0%
where the time goes in v1:
time: 207 us
  blocking collectives  105 us (51%)
  Pallas kernels  75.6 us (37%)
  other arithmetic  23.6 us (11%)
    pallas_call x1, Pallas kernels, make_sketch(): pl.pallas_call(sketch_kernel, grid=(nrows // target_tile,), in_specs=[pl....  57.4 us
    all_to_all x1, blocking collectives, shards(): lax.all_to_all(project(sketch, tiles, usable, row_devices), 'rows', 0, 0)  44.6 us
    all_to_all x1, blocking collectives, shards(): lax.all_to_all(partial.reshape(col_devices, -1, rank), 'cols', 0, 0)  28.2 us
    all_to_all x1, blocking collectives, shards(): lax.all_to_all(add_pieces(pieces), 'cols', 0, 0).reshape(rows_here, rank)  20.3 us
    another operation x3, other arithmetic, shards(): lower_factor = jnp.linalg.cholesky(gram_matrix)  12.4 us
    all_to_all x1, blocking collectives, shards(): gram_matrix = lax.all_to_all(band, 'cols', 0, 0).reshape(rank, rank)  11.8 us
    pallas_call x1, Pallas kernels, project(): pl.pallas_call(project_kernel, grid=(ncols // width,), in_specs=[pl.Block...  11.4 us
    another operation x2, other arithmetic, shards(): lax.linalg.triangular_solve(lower_factor, jnp.eye(rank, dtype=f32), left_...  10.5 us

profile of v1, /device:TPU:1, one launch (start us, length us, event | category | flops | bytes accessed | tf_op | source)
XLA Modules:
  0.0 206.5 jit_solution(3406478071375362060)
XLA Ops:
  0.6 0.8 fusion
  1.4 0.7 reshape.58.usable
  2.1 57.4 %sketch.1 = (bf16[2048,4096]{1,0:T(8,128)(2,1)}, bf16[2048,128]{1,0:T(8,128)(2,1)}) custom-call(f32[3,2048]{1,0:T(4,128)} %targets.1, f32[3,4096]{1,0:T(4,128)} %sources.1, f32[1,4096]{1,0:T(1,128)} %bitcast.18, f32[1,4096]{1,0:T(1,128)} %reshape.58.usable, bf16[4096,128]{1,0:T(8,128)(2,1)} %omega.1), custom_call_target="tpu_custom_call" | custom-call | tf_op jit(solution)/shard_map/sketch/pallas_call | solution.py:124
  59.5 28.2 %all_to_all.20.parts = bf16[16,128,128]{2,1,0:T(8,128)(2,1)} all-to-all(bf16[16,128,128]{2,1,0:T(8,128)(2,1)} %bitcast.17), channel_id=1, replica_groups=mesh['rows'=32,'cols'=16] {'cols'}, dimensions={0} | all-to-all | bytes 1048576 | tf_op jit(solution)/shard_map/all_to_all | solution.py:273
  87.7 1.9 pieces.1
  89.7 20.3 %all_to_all.21 = bf16[16,128,128]{2,1,0:T(8,128)(2,1)} all-to-all(bf16[16,128,128]{2,1,0:T(8,128)(2,1)} %pieces.1), channel_id=1, replica_groups=mesh['rows'=32,'cols'=16] {'cols'}, dimensions={0} | all-to-all | bytes 1048576 | tf_op jit(solution)/shard_map/all_to_all | solution.py:274
  110.0 11.4 %project.1 = bf16[32,160,128]{2,1,0:T(8,128)(2,1)} custom-call(bf16[2048,128]{1,0:T(8,128)(2,1)} %bitcast.14, bf16[2048,4096]{1,0:T(8,128)(2,1)} %get-tuple-element.7.tiles, f32[1,4096]{1,0:T(1,128)} %reshape.58.usable), custom_call_target="tpu_custom_call" | custom-call | tf_op jit(solution)/shard_map/project/pallas_call | solution.py:195
  121.3 44.6 %all_to_all.22.parts = bf16[32,160,128]{2,1,0:T(8,128)(2,1)} all-to-all(bf16[32,160,128]{2,1,0:T(8,128)(2,1)} %project.1), channel_id=1, replica_groups=mesh['rows'=32,'cols'=16] {'rows'}, dimensions={0} | all-to-all | bytes 2621440 | tf_op jit(solution)/shard_map/all_to_all | solution.py:275
  166.0 2.1 %fold.1 = (f32[128,128]{1,0:T(8,128)}, f32[16,8,128]{2,1,0:T(8,128)}) custom-call(bf16[32,160,128]{2,1,0:T(8,128)(2,1)} %all_to_all.22.parts), custom_call_target="tpu_custom_call" | custom-call | tf_op jit(solution)/shard_map/fold/pallas_call | solution.py:226
  168.1 11.8 %all_to_all.23 = f32[16,8,128]{2,1,0:T(8,128)S(1)} all-to-all(f32[16,8,128]{2,1,0:T(8,128)} %get-tuple-element.9), channel_id=1, replica_groups=mesh['rows'=32,'cols'=16] {'cols'}, dimensions={0} | all-to-all | bytes 131072 | tf_op jit(solution)/shard_map/all_to_all | solution.py:277
  179.9 0.1 copy.9
  180.0 11.7 %cholesky.17 = f32[128,128]{1,0:T(8,128)S(1)} custom-call(f32[128,128]{1,0:T(8,128)S(1)} %fusion.4), custom_call_target="Cholesky" | custom-call | tf_op jit(solution)/shard_map/jit(cholesky)/cholesky | solution.py:278
  191.8 0.6 compare_reduce_fusion
  192.4 0.7 fusion.1
  193.1 9.8 %custom-call.6 = f32[1,128,128]{1,2,0:T(8,128)S(1)} custom-call(f32[1,128,128]{2,1,0:T(8,128)S(1)} %fusion.1), custom_call_target="InvertDiagBlocksLowerTriangular" | custom-call | tf_op jit(solution)/shard_map/triangular_solve | solution.py:279
  202.9 0.9 fusion.2.inverse
  203.8 2.8 %finish.1 = (f32[2048,128]{1,0:T(8,128)}, f32[128,128]{1,0:T(8,128)}) custom-call(bf16[2048,128]{1,0:T(8,128)(2,1)} %bitcast.15, f32[128,128]{1,0:T(8,128)} %get-tuple-element.8.product, f32[128,128]{1,0:T(8,128)} %fusion.2.inverse), custom_call_target="tpu_custom_call" | custom-call | tf_op jit(solution)/shard_map/finish/pallas_call | solution.py:253
  (2 shorter events, 0.0 us)

commit v2 on v1

--- a/solution.py
+++ b/solution.py
@@ -14,7 +14,7 @@
 separation = 2.0
 turns = wave_number / (2.0 * math.pi)
 sine = (6.283164043875678, -41.33714231633244, 81.34076713243772, -70.99341720807224)
-target_tile = 256
+target_tile = 512
 source_tile = 512
 
 
@@ -43,14 +43,41 @@
 
 
 def sketch_kernel(targets, sources, weights, usable, omega, tiles, sketch,
-                  feature, tfeat, afeat, bfeat, masked, a_buf, b_buf, acc):
+                  feature, tfeat, afeat, bfeat, masked, a_even, b_even, k_even, a_odd, b_odd, k_odd, acc):
     step = pl.program_id(0)
-    ncols = sources.shape[1]
-    turns_n = ncols // source_tile
+    nrows, ncols = targets.shape[1], sources.shape[1]
+    per_step = nrows // target_tile
+    total = per_step * (ncols // source_tile)
+
+    def block(at, size):
+        return pl.ds(pl.multiple_of(at * size, size), size)
+
+    def distances(tile, a_buf, b_buf):
+        here = tfeat[block(lax.rem(tile, per_step), target_tile), :]
+        there = block(lax.div(tile, per_step), source_tile)
+        a_buf[...] = jnp.dot(here, afeat[:, there], preferred_element_type=f32)
+        b_buf[...] = jnp.dot(here, bfeat[:, there], preferred_element_type=f32)
+
+    def evaluate(tile, a_buf, b_buf, k_buf):
+        first = lax.rem(tile, per_step) * target_tile
+        for r in range(0, target_tile, 16):
+            over = lax.rsqrt(a_buf[r : r + 16, :])
+            turn = b_buf[r : r + 16, :] * over
+            away = 0.25 - jnp.abs(turn - jnp.round(turn))
+            square = away * away
+            c0, c1, c2, c3 = (turns * c for c in sine)
+            wave = ((c3 * square + c2) * square + c1) * square + c0
+            low = ((wave * away) * over).astype(bf16)
+            k_buf[r : r + 16, :] = low
+            tiles[pl.ds(pl.multiple_of(first + r, 16), 16), :] = low
+
+    def accumulate(tile, k_buf):
+        rows = block(lax.rem(tile, per_step), target_tile)
+        there = block(lax.div(tile, per_step), source_tile)
+        acc[rows, :] += jnp.dot(k_buf[...], masked[there, :], preferred_element_type=f32)
 
     @pl.when(step == 0)
     def _():
-        nrows = targets.shape[1]
         feature[...] = jnp.zeros_like(feature)
         tx = (targets[0:1, :] - (0.5 + 0.5 * separation)) * turns
         ty = (targets[1:2, :] - 0.5) * turns
@@ -74,47 +101,26 @@
             flag, jnp.ones((8, omega.shape[1]), bf16), (((0,), (0,)), ((), ())), preferred_element_type=f32
         )
         masked[...] = (omega[...].astype(f32) * column).astype(bf16)
-
-    here = tfeat[pl.ds(pl.multiple_of(step * target_tile, target_tile), target_tile), :]
-
-    def cols(j):
-        return pl.ds(pl.multiple_of(j * source_tile, source_tile), source_tile)
-
-    def distances(j):
-        slot = lax.rem(j, 2)
-        a_buf[slot] = jnp.dot(here, afeat[:, cols(j)], preferred_element_type=f32)
-        b_buf[slot] = jnp.dot(here, bfeat[:, cols(j)], preferred_element_type=f32)
-
-    def evaluate(j):
-        slot = lax.rem(j, 2)
-        for r in range(0, target_tile, 16):
-            a = a_buf[slot, r : r + 16, :]
-            b = b_buf[slot, r : r + 16, :]
-            over = lax.rsqrt(a)
-            turn = b * over
-            away = 0.25 - jnp.abs(turn - jnp.round(turn))
-            square = away * away
-            c0, c1, c2, c3 = (turns * c for c in sine)
-            wave = ((c3 * square + c2) * square + c1) * square + c0
-            tiles[r : r + 16, cols(j)] = ((wave * away) * over).astype(bf16)
-
-    def accumulate(j):
-        acc[...] += jnp.dot(tiles[:, cols(j)], masked[cols(j), :], preferred_element_type=f32)
-
-    acc[...] = jnp.zeros_like(acc)
-    distances(0)
-    distances(1)
-    evaluate(0)
-
-    def turn(j, carry):
-        distances(lax.rem(j + 1, turns_n))
-        evaluate(j)
-        accumulate(j - 1)
+        acc[...] = jnp.zeros_like(acc)
+        k_odd[...] = jnp.zeros_like(k_odd)
+        distances(0, a_even, b_even)
+
+    def pair(p, carry):
+        tile = step * per_step + 2 * p
+        distances(tile + 1, a_odd, b_odd)
+        evaluate(tile, a_even, b_even, k_even)
+        accumulate(jnp.maximum(tile - 1, 0), k_odd)
+        distances(jnp.minimum(tile + 2, total - 1), a_even, b_even)
+        evaluate(tile + 1, a_odd, b_odd, k_odd)
+        accumulate(tile, k_even)
         return carry
 
-    lax.fori_loop(1, turns_n, turn, 0)
-    accumulate(turns_n - 1)
-    sketch[...] = acc[...].astype(bf16)
+    lax.fori_loop(0, per_step // 2, pair, 0)
+
+    @pl.when(step == pl.num_programs(0) - 1)
+    def _():
+        accumulate(total - 1, k_odd)
+        sketch[...] = acc[...].astype(bf16)
 
 
 def make_sketch(targets, sources, weights, usable, omega):
@@ -123,7 +129,7 @@
     once = dict(pipeline_mode=pl.Buffered(1))
     return pl.pallas_call(
         sketch_kernel,
-        grid=(nrows // target_tile,),
+        grid=(ncols // source_tile,),
         in_specs=[
             pl.BlockSpec((3, nrows), whole, **once),
             pl.BlockSpec((3, ncols), whole, **once),
@@ -132,8 +138,8 @@
             pl.BlockSpec((ncols, rank), whole, **once),
         ],
         out_specs=[
-            pl.BlockSpec((target_tile, ncols), lambda i: (i, 0)),
-            pl.BlockSpec((target_tile, rank), lambda i: (i, 0)),
+            pl.BlockSpec((nrows, source_tile), lambda j: (0, j)),
+            pl.BlockSpec((nrows, rank), whole),
         ],
         out_shape=[
             jax.ShapeDtypeStruct((nrows, ncols), bf16),
@@ -145,9 +151,13 @@
             pltpu.VMEM((128, ncols), bf16),
             pltpu.VMEM((128, ncols), bf16),
             pltpu.VMEM((ncols, rank), bf16),
-            pltpu.VMEM((2, target_tile, source_tile), f32),
-            pltpu.VMEM((2, target_tile, source_tile), f32),
-            pltpu.VMEM((target_tile, rank), f32),
+            pltpu.VMEM((target_tile, source_tile), f32),
+            pltpu.VMEM((target_tile, source_tile), f32),
+            pltpu.VMEM((target_tile, source_tile), bf16),
+            pltpu.VMEM((target_tile, source_tile), f32),
+            pltpu.VMEM((target_tile, source_tile), f32),
+            pltpu.VMEM((target_tile, source_tile), bf16),
+            pltpu.VMEM((nrows, rank), f32),
         ],
         name="sketch",
     )(targets, sources, weights, usable, omega)
@@ -157,14 +167,13 @@
     total = parts[0].astype(f32)
     for k in range(1, parts.shape[0]):
         total += parts[k].astype(f32)
-    low = total.astype(bf16)
     for k in range(out.shape[0]):
-        out[k] = low
+        out[k] = total
 
 
 def add_pieces(parts):
     return pl.pallas_call(
-        piece_kernel, out_shape=jax.ShapeDtypeStruct(parts.shape, bf16), name="pieces"
+        piece_kernel, out_shape=jax.ShapeDtypeStruct(parts.shape, f32), name="pieces"
     )(parts)
 
 
@@ -174,17 +183,23 @@
 
     @pl.when(pl.program_id(0) == 0)
     def _():
-        flipped[...] = sketch[...].astype(f32).T.astype(bf16)
-        gram[...] = jnp.dot(flipped[...], sketch[...], preferred_element_type=f32)
+        whole = sketch[...]
+        upper = whole.astype(bf16)
+        lower = (whole - upper.astype(f32)).astype(bf16)
+        contract = (((0,), (0,)), ((), ()))
+        flipped[...] = upper.astype(f32).T.astype(bf16)
+        cross = lax.dot_general(upper, lower, contract, preferred_element_type=f32)
+        gram[...] = lax.dot_general(lower, lower, contract, preferred_element_type=f32) + (cross + cross.T)
+        gram[...] += jnp.dot(flipped[...], upper, preferred_element_type=f32)
 
     product = jnp.dot(flipped[...], tiles[...], preferred_element_type=f32)
     product = (product * usable[...]).astype(bf16)
     first = pl.multiple_of(lax.axis_index("cols") * band, band)
     own = jnp.concatenate([part.astype(f32) for part in thirds(gram[pl.ds(first, band), :])], axis=0)
-    own = jnp.concatenate([own, jnp.zeros((32 - 3 * band, rank), f32)], axis=0).astype(bf16)
+    own = own.astype(bf16)
     for k in range(out.shape[0]):
         out[k, 0:rank, :] = product[:, 128 * k : 128 * k + 128]
-        out[k, rank : rank + 32, :] = own
+        out[k, rank:, :] = own
 
 
 def project(sketch, tiles, usable, row_devices):
@@ -200,8 +215,8 @@
             pl.BlockSpec((nrows, width), lambda j: (0, j)),
             pl.BlockSpec((1, width), lambda j: (0, j)),
         ],
-        out_specs=pl.BlockSpec((dests, rank + 32, 128), lambda j: (j, 0, 0)),
-        out_shape=jax.ShapeDtypeStruct((row_devices, rank + 32, 128), bf16),
+        out_specs=pl.BlockSpec((dests, rank + 24, 128), lambda j: (j, 0, 0)),
+        out_shape=jax.ShapeDtypeStruct((row_devices, rank + 24, 128), bf16),
         scratch_shapes=[pltpu.VMEM((rank, nrows), bf16), pltpu.VMEM((rank, rank), f32)],
         name="project",
     )(sketch, tiles, usable)
@@ -222,7 +237,7 @@
 
 
 def fold(parts, col_devices):
-    rank = parts.shape[1] - 32
+    rank = parts.shape[1] - 24
     return pl.pallas_call(
         fold_kernel,
         out_shape=[
@@ -233,13 +248,45 @@
     )(parts)
 
 
-def finish_kernel(scale, sketch, product, inverse, basis, projected):
+def inverse_factor(bands):
+    count, _, rank = bands.shape
+    at_row = lax.broadcasted_iota(jnp.int32, (8, rank), 0)
+    at_col = lax.broadcasted_iota(jnp.int32, (8, rank), 1)
+    left = [bands[i] for i in range(count)]
+    right = [jnp.where(at_col == at_row + 8 * i, 1.0, 0.0) for i in range(count)]
+    for k in range(rank):
+        block, r = divmod(k, 8)
+        row = jnp.broadcast_to(left[block][r : r + 1, :], (8, rank))
+        other = jnp.broadcast_to(right[block][r : r + 1, :], (8, rank))
+        pivot = 1.0 / jnp.broadcast_to(row[:, k : k + 1], (8, rank))
+        for i in range(block, count):
+            if i == block and r == 7:
+                continue
+            factor = jnp.broadcast_to(left[i][:, k : k + 1], (8, rank)) * pivot
+            if i == block:
+                factor = jnp.where(at_row > r, factor, 0.0)
+            left[i] = left[i] - factor * row
+            right[i] = right[i] - factor * other
+    out = []
+    for i in range(count):
+        diagonal = jnp.sum(jnp.where(at_col == at_row + 8 * i, left[i], 0.0), axis=1, keepdims=True)
+        out.append(right[i] * lax.rsqrt(jnp.broadcast_to(diagonal, (8, rank))))
+    return out
+
+
+def finish_kernel(scale, sketch, product, bands, basis, projected, inverse):
+    for i, rows in enumerate(inverse_factor(bands)):
+        inverse[8 * i : 8 * i + 8, :] = rows
+    contract = (((1,), (1,)), ((), ()))
     high, middle, low = thirds(inverse[...] * scale)
-    contract = (((1,), (1,)), ((), ()))
-    rows = sketch[...]
-    total = lax.dot_general(rows, low, contract, preferred_element_type=f32)
-    total += lax.dot_general(rows, middle, contract, preferred_element_type=f32)
-    basis[...] = total + lax.dot_general(rows, high, contract, preferred_element_type=f32)
+    whole = sketch[...]
+    upper = whole.astype(bf16)
+    lower = (whole - upper.astype(f32)).astype(bf16)
+    total = lax.dot_general(upper, low, contract, preferred_element_type=f32)
+    total += lax.dot_general(lower, middle, contract, preferred_element_type=f32)
+    total += lax.dot_general(lower, high, contract, preferred_element_type=f32)
+    total += lax.dot_general(upper, middle, contract, preferred_element_type=f32)
+    basis[...] = total + lax.dot_general(upper, high, contract, preferred_element_type=f32)
     projected[...] = lax.dot_general(
         product[...].T,
         inverse[...],
@@ -249,15 +296,16 @@
     )
 
 
-def finish(sketch, product, inverse, scale):
+def finish(sketch, product, bands, scale):
     return pl.pallas_call(
         functools.partial(finish_kernel, scale),
         out_shape=[
             jax.ShapeDtypeStruct(sketch.shape, f32),
             jax.ShapeDtypeStruct(product.shape, f32),
         ],
+        scratch_shapes=[pltpu.VMEM(product.shape, f32)],
         name="finish",
-    )(sketch, product, inverse)
+    )(sketch, product, bands)
 
 
 def shards(targets, sources, weights, counts, omega):
@@ -274,10 +322,8 @@
     sketch = lax.all_to_all(add_pieces(pieces), "cols", 0, 0).reshape(rows_here, rank)
     terms = lax.all_to_all(project(sketch, tiles, usable, row_devices), "rows", 0, 0)
     product, band = fold(terms, col_devices)
-    gram_matrix = lax.all_to_all(band, "cols", 0, 0).reshape(rank, rank)
-    lower_factor = jnp.linalg.cholesky(gram_matrix)
-    inverse = lax.linalg.triangular_solve(lower_factor, jnp.eye(rank, dtype=f32), left_side=True, lower=True)
-    return finish(sketch, product, inverse, math.sqrt(rows_here * row_devices))
+    bands = lax.all_to_all(band, "cols", 0, 0)
+    return finish(sketch, product, bands, math.sqrt(rows_here * row_devices))
 
 
 def solution(mesh):

time: 207 us -> 185 us (0.89)
  other arithmetic: 23.6 us -> 0.78 us
  blocking collectives: 105 us -> 116 us
  Pallas kernels: 75.6 us -> 66.9 us
    pallas_call x1, Pallas kernels: 57.4 us -> 30.7 us  [make_sketch(): pl.pallas_call(sketch_kernel, grid=(ncols // source_tile,), in_specs=[pl....]
    another operation x5 -> x0, other arithmetic: 22.9 us -> none  [the longest x3 12.4 us: shards(): lower_factor = jnp.linalg.cholesky(gram_matrix)]
    pallas_call x1, Pallas kernels: 2.76 us -> 20.1 us  [finish(): pl.pallas_call(functools.partial(finish_kernel, scale), out_shape=[jax.Sh...]
    all_to_all x1, blocking collectives: 20.3 us -> 31.5 us  [shards(): lax.all_to_all(add_pieces(pieces), 'cols', 0, 0).reshape(rows_here, rank)]
where the time goes in v2:
time: 185 us
  blocking collectives  116 us (63%)
  Pallas kernels  66.9 us (36%)
    all_to_all x1, blocking collectives, shards(): lax.all_to_all(project(sketch, tiles, usable, row_devices), 'rows', 0, 0)  43.6 us
    all_to_all x1, blocking collectives, shards(): lax.all_to_all(add_pieces(pieces), 'cols', 0, 0).reshape(rows_here, rank)  31.5 us
    pallas_call x1, Pallas kernels, make_sketch(): pl.pallas_call(sketch_kernel, grid=(ncols // source_tile,), in_specs=[pl....  30.7 us
    all_to_all x1, blocking collectives, shards(): lax.all_to_all(partial.reshape(col_devices, -1, rank), 'cols', 0, 0)  28.2 us
    pallas_call x1, Pallas kernels, finish(): pl.pallas_call(functools.partial(finish_kernel, scale), out_shape=[jax.Sh...  20.1 us
    all_to_all x1, blocking collectives, shards(): bands = lax.all_to_all(band, 'cols', 0, 0)  12.2 us
    pallas_call x1, Pallas kernels, project(): pl.pallas_call(project_kernel, grid=(ncols // width,), in_specs=[pl.Block...  11.8 us

profile of v2, /device:TPU:1, one launch (start us, length us, event | category | flops | bytes accessed | tf_op | source)
XLA Modules:
  0.0 184.6 jit_solution(8410531877628830565)
XLA Ops:
  0.6 0.8 fusion
  1.4 0.7 reshape.45.usable
  2.1 30.7 %sketch.1 = (bf16[2048,4096]{1,0:T(8,128)(2,1)}, bf16[2048,128]{1,0:T(8,128)(2,1)}) custom-call(f32[3,2048]{1,0:T(4,128)} %targets.1, f32[3,4096]{1,0:T(4,128)} %sources.1, f32[1,4096]{1,0:T(1,128)} %bitcast.6, f32[1,4096]{1,0:T(1,128)} %reshape.45.usable, bf16[4096,128]{1,0:T(8,128)(2,1)} %omega.1), custom_call_target="tpu_custom_call" | custom-call | tf_op jit(solution)/shard_map/sketch/pallas_call | solution.py:130
  32.8 28.2 %all_to_all.20.parts = bf16[16,128,128]{2,1,0:T(8,128)(2,1)} all-to-all(bf16[16,128,128]{2,1,0:T(8,128)(2,1)} %bitcast.5), channel_id=1, replica_groups=mesh['rows'=32,'cols'=16] {'cols'}, dimensions={0} | all-to-all | bytes 1048576 | tf_op jit(solution)/shard_map/all_to_all | solution.py:321
  61.0 2.1 %pieces.1 = f32[16,128,128]{2,1,0:T(8,128)} custom-call(bf16[16,128,128]{2,1,0:T(8,128)(2,1)} %all_to_all.20.parts), custom_call_target="tpu_custom_call" | custom-call | tf_op jit(solution)/shard_map/pieces/pallas_call | solution.py:175
  63.2 31.5 %all_to_all.21 = f32[16,128,128]{2,1,0:T(8,128)} all-to-all(f32[16,128,128]{2,1,0:T(8,128)} %pieces.1), channel_id=1, replica_groups=mesh['rows'=32,'cols'=16] {'cols'}, dimensions={0} | all-to-all | bytes 2097152 | tf_op jit(solution)/shard_map/all_to_all | solution.py:322
  94.7 11.8 %project.1 = bf16[32,152,128]{2,1,0:T(8,128)(2,1)} custom-call(f32[2048,128]{1,0:T(8,128)} %bitcast.3, bf16[2048,4096]{1,0:T(8,128)(2,1)} %get-tuple-element.7.tiles, f32[1,4096]{1,0:T(1,128)} %reshape.45.usable), custom_call_target="tpu_custom_call" | custom-call | tf_op jit(solution)/shard_map/project/pallas_call | solution.py:210
  106.6 43.6 %all_to_all.22.parts = bf16[32,152,128]{2,1,0:T(8,128)(2,1)} all-to-all(bf16[32,152,128]{2,1,0:T(8,128)(2,1)} %project.1), channel_id=1, replica_groups=mesh['rows'=32,'cols'=16] {'rows'}, dimensions={0} | all-to-all | bytes 2490368 | tf_op jit(solution)/shard_map/all_to_all | solution.py:323
  150.2 2.1 %fold.1 = (f32[128,128]{1,0:T(8,128)}, f32[16,8,128]{2,1,0:T(8,128)}) custom-call(bf16[32,152,128]{2,1,0:T(8,128)(2,1)} %all_to_all.22.parts), custom_call_target="tpu_custom_call" | custom-call | tf_op jit(solution)/shard_map/fold/pallas_call | solution.py:241
  152.3 12.2 %all_to_all.23.bands = f32[16,8,128]{2,1,0:T(8,128)} all-to-all(f32[16,8,128]{2,1,0:T(8,128)} %get-tuple-element.9), channel_id=1, replica_groups=mesh['rows'=32,'cols'=16] {'cols'}, dimensions={0} | all-to-all | bytes 131072 | tf_op jit(solution)/shard_map/all_to_all | solution.py:325
  164.5 20.1 %finish.1 = (f32[2048,128]{1,0:T(8,128)}, f32[128,128]{1,0:T(8,128)}) custom-call(f32[2048,128]{1,0:T(8,128)} %bitcast.4, f32[128,128]{1,0:T(8,128)} %get-tuple-element.8.product, f32[16,8,128]{2,1,0:T(8,128)} %all_to_all.23.bands), custom_call_target="tpu_custom_call" | custom-call | tf_op jit(solution)/shard_map/finish/pallas_call | solution.py:300

commit v3 on v2

--- a/solution.py
+++ b/solution.py
@@ -159,7 +159,7 @@
             pltpu.VMEM((target_tile, source_tile), bf16),
             pltpu.VMEM((nrows, rank), f32),
         ],
-        name="sketch",
+        name="sketch", compiler_params=pltpu.CompilerParams(vmem_limit_bytes=24 << 20),
     )(targets, sources, weights, usable, omega)
 
 
@@ -173,7 +173,7 @@
 
 def add_pieces(parts):
     return pl.pallas_call(
-        piece_kernel, out_shape=jax.ShapeDtypeStruct(parts.shape, f32), name="pieces"
+        piece_kernel, out_shape=jax.ShapeDtypeStruct(parts.shape, f32), name="pieces", compiler_params=pltpu.CompilerParams(vmem_limit_bytes=6 << 20)
     )(parts)
 
 
@@ -218,7 +218,7 @@
         out_specs=pl.BlockSpec((dests, rank + 24, 128), lambda j: (j, 0, 0)),
         out_shape=jax.ShapeDtypeStruct((row_devices, rank + 24, 128), bf16),
         scratch_shapes=[pltpu.VMEM((rank, nrows), bf16), pltpu.VMEM((rank, rank), f32)],
-        name="project",
+        name="project", compiler_params=pltpu.CompilerParams(vmem_limit_bytes=14 << 20),
     )(sketch, tiles, usable)
 
 
@@ -244,33 +244,52 @@
             jax.ShapeDtypeStruct((rank, rank), f32),
             jax.ShapeDtypeStruct((col_devices, rank // col_devices, rank), f32),
         ],
-        name="fold",
+        name="fold", compiler_params=pltpu.CompilerParams(vmem_limit_bytes=6 << 20),
     )(parts)
 
 
 def inverse_factor(bands):
     count, _, rank = bands.shape
-    at_row = lax.broadcasted_iota(jnp.int32, (8, rank), 0)
-    at_col = lax.broadcasted_iota(jnp.int32, (8, rank), 1)
+    shape = (8, rank)
+    at_row = lax.broadcasted_iota(jnp.int32, shape, 0)
+    at_col = lax.broadcasted_iota(jnp.int32, shape, 1)
     left = [bands[i] for i in range(count)]
     right = [jnp.where(at_col == at_row + 8 * i, 1.0, 0.0) for i in range(count)]
-    for k in range(rank):
+    inside = at_row < 8
+
+    def along_lanes(values, k):
+        return jnp.where(inside, jnp.broadcast_to(values[:, k : k + 1], shape), 0.0)
+
+    def along_rows(values, r):
+        return jnp.broadcast_to(values[r : r + 1, :], shape)
+
+    for k in range(0, rank, 2):
         block, r = divmod(k, 8)
-        row = jnp.broadcast_to(left[block][r : r + 1, :], (8, rank))
-        other = jnp.broadcast_to(right[block][r : r + 1, :], (8, rank))
-        pivot = 1.0 / jnp.broadcast_to(row[:, k : k + 1], (8, rank))
+        first = [along_lanes(left[i], k) for i in range(block, count)]
+        second = [along_lanes(left[i], k + 1) for i in range(block, count)]
+        a, b, c = along_rows(first[0], r), along_rows(first[0], r + 1), along_rows(second[0], r + 1)
+        scale = 1.0 / (a * c - b * b)
+        a_s, b_s, c_s = a * scale, b * scale, c * scale
+        upper, lower = along_rows(left[block], r), along_rows(left[block], r + 1)
+        upper_r, lower_r = along_rows(right[block], r), along_rows(right[block], r + 1)
         for i in range(block, count):
-            if i == block and r == 7:
+            if i == block and r == 6:
                 continue
-            factor = jnp.broadcast_to(left[i][:, k : k + 1], (8, rank)) * pivot
+            one, two = first[i - block], second[i - block]
+            u = one * c_s - two * b_s
+            v = two * a_s - one * b_s
             if i == block:
-                factor = jnp.where(at_row > r, factor, 0.0)
-            left[i] = left[i] - factor * row
-            right[i] = right[i] - factor * other
+                u = jnp.where(at_row > r + 1, u, 0.0)
+                v = jnp.where(at_row > r + 1, v, 0.0)
+            left[i] = left[i] - (u * upper + v * lower)
+            right[i] = right[i] - (u * upper_r + v * lower_r)
+        ratio = jnp.where(at_row == r + 1, b * (1.0 / a), 0.0)
+        left[block] = left[block] - ratio * upper
+        right[block] = right[block] - ratio * upper_r
     out = []
     for i in range(count):
         diagonal = jnp.sum(jnp.where(at_col == at_row + 8 * i, left[i], 0.0), axis=1, keepdims=True)
-        out.append(right[i] * lax.rsqrt(jnp.broadcast_to(diagonal, (8, rank))))
+        out.append(right[i] * lax.rsqrt(jnp.broadcast_to(diagonal, shape)))
     return out
 
 
@@ -304,7 +323,7 @@
             jax.ShapeDtypeStruct(product.shape, f32),
         ],
         scratch_shapes=[pltpu.VMEM(product.shape, f32)],
-        name="finish",
+        name="finish", compiler_params=pltpu.CompilerParams(vmem_limit_bytes=8 << 20),
     )(sketch, product, bands)
 
 

time: 185 us -> 163 us (0.88)
  Pallas kernels: 66.9 us -> 43.2 us
  local copies, waits for them, and re-layouts: 0.72 us -> 3.64 us
  blocking collectives: 116 us -> 114 us
    pallas_call x1, Pallas kernels: 20.1 us -> 7.99 us  [finish(): pl.pallas_call(functools.partial(finish_kernel, scale), out_shape=[jax.Sh...]
    pallas_call x1, Pallas kernels: 11.8 us -> 5.69 us  [project(): pl.pallas_call(project_kernel, grid=(ncols // width,), in_specs=[pl.Block...]
    unnamed x0 -> x8, local copies, waits for them, and re-layouts: none -> 3.53 us
    pallas_call x1, Pallas kernels: 2.14 us -> 0.12 us  [add_pieces(): pl.pallas_call(piece_kernel, out_shape=jax.ShapeDtypeStruct(parts.shape,...]
    pallas_call x1, Pallas kernels: 2.11 us -> 0.18 us  [fold(): pl.pallas_call(fold_kernel, out_shape=[jax.ShapeDtypeStruct((rank, rank),...]
where the time goes in v3:
time: 163 us; the launch traced here: 162 us
  blocking collectives  114 us (70%)
  Pallas kernels  43.2 us (27%)
  local copies, waits for them, and re-layouts  3.64 us (2%)
    all_to_all x1, blocking collectives, shards(): lax.all_to_all(project(sketch, tiles, usable, row_devices), 'rows', 0, 0)  44.6 us
    all_to_all x1, blocking collectives, shards(): lax.all_to_all(add_pieces(pieces), 'cols', 0, 0).reshape(rows_here, rank)  31.2 us
    pallas_call x1, Pallas kernels, make_sketch(): pl.pallas_call(sketch_kernel, grid=(ncols // source_tile,), in_specs=[pl....  29.2 us
    all_to_all x1, blocking collectives, shards(): lax.all_to_all(partial.reshape(col_devices, -1, rank), 'cols', 0, 0)  26.6 us
    all_to_all x1, blocking collectives, shards(): bands = lax.all_to_all(band, 'cols', 0, 0)  11.9 us
    pallas_call x1, Pallas kernels, finish(): pl.pallas_call(functools.partial(finish_kernel, scale), out_shape=[jax.Sh...  7.99 us
    pallas_call x1, Pallas kernels, project(): pl.pallas_call(project_kernel, grid=(ncols // width,), in_specs=[pl.Block...  5.69 us
    unnamed x8, local copies, waits for them, and re-layouts  3.53 us

profile of v3, /device:TPU:1, one launch (start us, length us, event | category | flops | bytes accessed | tf_op | source)
XLA Modules:
  0.0 162.5 jit_solution(13054111678411420274)
XLA Ops:
  0.6 0.8 fusion
  1.4 0.1 reshape.45.usable
  1.5 0.0 copy-start
  1.5 1.2 copy-done
  2.8 0.0 copy-start.1
  2.8 0.8 copy-done.1
  3.6 0.0 copy-start.2
  3.6 0.8 copy-done.2
  4.4 0.0 copy-start.3
  4.4 0.7 copy-done.3
  5.1 29.2 %sketch.1 = (bf16[2048,4096]{1,0:T(8,128)(2,1)S(1)}, bf16[2048,128]{1,0:T(8,128)(2,1)S(1)}) custom-call(f32[3,2048]{1,0:T(4,128)S(1)} %copy-done.2, f32[3,4096]{1,0:T(4,128)S(1)} %copy-done.1, f32[1,4096]{1,0:T(1,128)S(1)} %bitcast.6, f32[1,4096]{1,0:T(1,128)S(1)} %reshape.45.usable, bf16[4096,128]{1,0:T(8,128)(2,1)S(1)} %copy-done), custom_call_target="tpu_custom_call" | custom-call | tf_op jit(solution)/shard_map/sketch/pallas_call | solution.py:130
  34.3 26.6 %all_to_all.20.parts = bf16[16,128,128]{2,1,0:T(8,128)(2,1)S(1)} all-to-all(bf16[16,128,128]{2,1,0:T(8,128)(2,1)S(1)} %bitcast.5), channel_id=1, replica_groups=mesh['rows'=32,'cols'=16] {'cols'}, dimensions={0} | all-to-all | bytes 1048576 | tf_op jit(solution)/shard_map/all_to_all | solution.py:340
  60.9 0.1 pieces.1
  61.0 31.2 %all_to_all.21 = f32[16,128,128]{2,1,0:T(8,128)S(1)} all-to-all(f32[16,128,128]{2,1,0:T(8,128)S(1)} %pieces.1), channel_id=1, replica_groups=mesh['rows'=32,'cols'=16] {'cols'}, dimensions={0} | all-to-all | bytes 2097152 | tf_op jit(solution)/shard_map/all_to_all | solution.py:341
  92.2 5.7 %project.1 = bf16[32,152,128]{2,1,0:T(8,128)(2,1)S(1)} custom-call(f32[2048,128]{1,0:T(8,128)S(1)} %bitcast.3, bf16[2048,4096]{1,0:T(8,128)(2,1)S(1)} %get-tuple-element.7.tiles, f32[1,4096]{1,0:T(1,128)S(1)} %reshape.45.usable), custom_call_target="tpu_custom_call" | custom-call | tf_op jit(solution)/shard_map/project/pallas_call | solution.py:210
  97.9 44.6 %all_to_all.22.parts = bf16[32,152,128]{2,1,0:T(8,128)(2,1)S(1)} all-to-all(bf16[32,152,128]{2,1,0:T(8,128)(2,1)S(1)} %project.1), channel_id=1, replica_groups=mesh['rows'=32,'cols'=16] {'rows'}, dimensions={0} | all-to-all | bytes 2490368 | tf_op jit(solution)/shard_map/all_to_all | solution.py:342
  142.4 0.2 fold.1
  142.6 11.9 %all_to_all.23.bands = f32[16,8,128]{2,1,0:T(8,128)S(1)} all-to-all(f32[16,8,128]{2,1,0:T(8,128)S(1)} %get-tuple-element.9), channel_id=1, replica_groups=mesh['rows'=32,'cols'=16] {'cols'}, dimensions={0} | all-to-all | bytes 131072 | tf_op jit(solution)/shard_map/all_to_all | solution.py:344
  154.5 8.0 %finish.1 = (f32[2048,128]{1,0:T(8,128)}, f32[128,128]{1,0:T(8,128)}) custom-call(f32[2048,128]{1,0:T(8,128)S(1)} %bitcast.4, f32[128,128]{1,0:T(8,128)S(1)} %get-tuple-element.8.product, f32[16,8,128]{2,1,0:T(8,128)S(1)} %all_to_all.23.bands), custom_call_target="tpu_custom_call" | custom-call | tf_op jit(solution)/shard_map/finish/pallas_call | solution.py:319
Async XLA Ops:
  1.5 1.2 copy-start
  2.8 0.8 copy-start.1
  3.6 0.8 copy-start.2
  4.4 0.7 copy-start.3

commit v4 on v3

--- a/solution.py
+++ b/solution.py
@@ -42,8 +42,13 @@
             ref[8 * k : 8 * k + 8, :] = parts[p if outer else q]
 
 
-def sketch_kernel(targets, sources, weights, usable, omega, tiles, sketch,
-                  feature, tfeat, afeat, bfeat, masked, a_even, b_even, k_even, a_odd, b_odd, k_odd, acc):
+def halves():
+    own = lax.rem(lax.axis_index("cols"), 2)
+    return own, 1 - own
+
+
+def sketch_kernel(targets_in, sources_in, weights_in, counts_in, omega_in, tiles, sketch, usable,
+                  targets, sources, weights, counts, omega, arrived, feature, tfeat, afeat, bfeat, masked, a_even, b_even, k_even, a_odd, b_odd, k_odd, acc):
     step = pl.program_id(0)
     nrows, ncols = targets.shape[1], sources.shape[1]
     per_step = nrows // target_tile
@@ -76,17 +81,35 @@
         there = block(lax.div(tile, per_step), source_tile)
         acc[rows, :] += jnp.dot(k_buf[...], masked[there, :], preferred_element_type=f32)
 
+    own, other = halves()
+    half = nrows // 2
+    pieces, rank = sketch.shape[0], sketch.shape[2]
+    share = half // pieces
+
     @pl.when(step == 0)
     def _():
+        moves = [
+            pltpu.make_async_copy(source, target, arrived.at[k])
+            for k, (source, target) in enumerate(
+                [(targets_in, targets), (sources_in, sources), (weights_in, weights), (counts_in, counts), (omega_in, omega)]
+            )
+        ]
+        for move in moves:
+            move.start()
         feature[...] = jnp.zeros_like(feature)
+        moves[0].wait()
         tx = (targets[0:1, :] - (0.5 + 0.5 * separation)) * turns
         ty = (targets[1:2, :] - 0.5) * turns
         tz = (targets[2:3, :] - 0.5) * turns
         rows = [tx, ty, tz, tx * tx + ty * ty + tz * tz, jnp.ones_like(tx)]
         view = feature.at[:, 0:nrows]
         put_thirds(view, pick_rows(rows, (8, nrows)), True)
-        for k in range(nrows // 128):
-            tfeat[128 * k : 128 * k + 128, :] = feature[:, 128 * k : 128 * k + 128].T.astype(bf16)
+        for k in range(pieces):
+            block_rows = feature[:, 2 * share * k : 2 * share * (k + 1)].T.astype(bf16)
+            tfeat[pl.ds(pl.multiple_of(own * half + share * k, share), share), :] = block_rows[0:share]
+            tfeat[pl.ds(pl.multiple_of(other * half + share * k, share), share), :] = block_rows[share : 2 * share]
+        for move in moves[1:4]:
+            move.wait()
         sx = (sources[0:1, :] + (0.5 * separation - 0.5)) * turns
         sy = (sources[1:2, :] - 0.5) * turns
         sz = (sources[2:3, :] - 0.5) * turns
@@ -96,14 +119,28 @@
             rows = [-2.0 * sx * scale, -2.0 * sy * scale, -2.0 * sz * scale, scale, norm * scale]
             put_thirds(feature, pick_rows(rows, (8, ncols)), False)
             ref[...] = feature[...].astype(bf16)
-        flag = pick_rows([usable[...]], (8, ncols)).astype(bf16)
-        column = lax.dot_general(
-            flag, jnp.ones((8, omega.shape[1]), bf16), (((0,), (0,)), ((), ())), preferred_element_type=f32
-        )
-        masked[...] = (omega[...].astype(f32) * column).astype(bf16)
+        panels = counts.shape[1]
+        size = ncols // panels
+        span = 128 // size
+        shape = (ncols // 128, panels)
+        mine = lax.shift_right_logical(lax.broadcasted_iota(jnp.int32, shape, 1), span.bit_length() - 1) == lax.broadcasted_iota(jnp.int32, shape, 0)
+        chosen = jnp.where(mine, jnp.broadcast_to(counts[...].astype(f32), shape), 0.0).astype(bf16)
+        shape = (panels, 128)
+        spread = (lax.broadcasted_iota(jnp.int32, shape, 0) & (span - 1)) == lax.shift_right_logical(lax.broadcasted_iota(jnp.int32, shape, 1), size.bit_length() - 1)
+        filled = jnp.dot(chosen, jnp.where(spread, 1.0, 0.0).astype(bf16), preferred_element_type=f32)
+        lane = (lax.broadcasted_iota(jnp.int32, filled.shape, 1) & (size - 1)).astype(f32)
+        flags = jnp.where(lane < filled, 1.0, 0.0)
+        for k in range(ncols // 128):
+            usable[0:1, 128 * k : 128 * k + 128] = flags[k : k + 1, :]
+        moves[4].wait()
+        distances(0, a_even, b_even)
+        columns = flags.T
+        for k in range(ncols // 128):
+            rows = slice(128 * k, 128 * k + 128)
+            flag = jnp.broadcast_to(columns[:, k : k + 1], (128, rank))
+            masked[rows, :] = (omega[rows, :].astype(f32) * flag).astype(bf16)
         acc[...] = jnp.zeros_like(acc)
         k_odd[...] = jnp.zeros_like(k_odd)
-        distances(0, a_even, b_even)
 
     def pair(p, carry):
         tile = step * per_step + 2 * p
@@ -120,32 +157,36 @@
     @pl.when(step == pl.num_programs(0) - 1)
     def _():
         accumulate(total - 1, k_odd)
-        sketch[...] = acc[...].astype(bf16)
-
-
-def make_sketch(targets, sources, weights, usable, omega):
+        for k in range(pieces):
+            for part, keeper in ((0, own), (1, other)):
+                rows = pl.ds(pl.multiple_of(keeper * half + share * k, share), share)
+                sketch[k, part * share : (part + 1) * share, :] = acc[rows, :].astype(bf16)
+
+
+def make_sketch(targets, sources, weights, counts, omega, col_devices):
     nrows, ncols, rank = targets.shape[1], sources.shape[1], omega.shape[1]
-    whole = lambda i: (0, 0)
-    once = dict(pipeline_mode=pl.Buffered(1))
+    operands = [pltpu.with_memory_space_constraint(x, pltpu.HBM) for x in (targets, sources, weights, counts, omega)]
     return pl.pallas_call(
         sketch_kernel,
         grid=(ncols // source_tile,),
-        in_specs=[
-            pl.BlockSpec((3, nrows), whole, **once),
-            pl.BlockSpec((3, ncols), whole, **once),
-            pl.BlockSpec((1, ncols), whole, **once),
-            pl.BlockSpec((1, ncols), whole, **once),
-            pl.BlockSpec((ncols, rank), whole, **once),
-        ],
+        in_specs=[pl.BlockSpec(memory_space=pltpu.HBM)] * 5,
         out_specs=[
             pl.BlockSpec((nrows, source_tile), lambda j: (0, j)),
-            pl.BlockSpec((nrows, rank), whole),
+            pl.BlockSpec((col_devices, nrows // col_devices, rank), lambda j: (0, 0, 0)),
+            pl.BlockSpec((1, ncols), lambda j: (0, 0)),
         ],
         out_shape=[
             jax.ShapeDtypeStruct((nrows, ncols), bf16),
-            jax.ShapeDtypeStruct((nrows, rank), bf16),
+            jax.ShapeDtypeStruct((col_devices, nrows // col_devices, rank), bf16),
+            jax.ShapeDtypeStruct((1, ncols), f32),
         ],
         scratch_shapes=[
+            pltpu.VMEM((3, nrows), f32),
+            pltpu.VMEM((3, ncols), f32),
+            pltpu.VMEM((1, ncols), f32),
+            pltpu.VMEM(counts.shape, jnp.int32),
+            pltpu.VMEM((ncols, rank), bf16),
+            pltpu.SemaphoreType.DMA((5,)),
             pltpu.VMEM((128, ncols), f32),
             pltpu.VMEM((nrows, 128), bf16),
             pltpu.VMEM((128, ncols), bf16),
@@ -160,37 +201,46 @@
             pltpu.VMEM((nrows, rank), f32),
         ],
         name="sketch", compiler_params=pltpu.CompilerParams(vmem_limit_bytes=24 << 20),
-    )(targets, sources, weights, usable, omega)
+    )(*operands)
 
 
 def piece_kernel(parts, out):
     total = parts[0].astype(f32)
     for k in range(1, parts.shape[0]):
         total += parts[k].astype(f32)
+    share = out.shape[1]
     for k in range(out.shape[0]):
-        out[k] = total
+        out[k] = total[0:share] if k % 2 == 0 else total[share : 2 * share]
 
 
 def add_pieces(parts):
+    count, rows, rank = parts.shape
     return pl.pallas_call(
-        piece_kernel, out_shape=jax.ShapeDtypeStruct(parts.shape, f32), name="pieces", compiler_params=pltpu.CompilerParams(vmem_limit_bytes=6 << 20)
+        piece_kernel,
+        out_shape=jax.ShapeDtypeStruct((count, rows // 2, rank), f32),
+        name="pieces", compiler_params=pltpu.CompilerParams(vmem_limit_bytes=6 << 20),
     )(parts)
 
 
-def project_kernel(sketch, tiles, usable, out, flipped, gram):
-    rank = sketch.shape[1]
+def project_kernel(near, far, tiles, usable, out, flipped, gram):
+    half, rank = near.shape
     band = gram.shape[0] // lax.axis_size("cols")
 
     @pl.when(pl.program_id(0) == 0)
     def _():
-        whole = sketch[...]
-        upper = whole.astype(bf16)
-        lower = (whole - upper.astype(f32)).astype(bf16)
         contract = (((0,), (0,)), ((), ()))
-        flipped[...] = upper.astype(f32).T.astype(bf16)
-        cross = lax.dot_general(upper, lower, contract, preferred_element_type=f32)
-        gram[...] = lax.dot_general(lower, lower, contract, preferred_element_type=f32) + (cross + cross.T)
-        gram[...] += jnp.dot(flipped[...], upper, preferred_element_type=f32)
+        total = jnp.zeros_like(gram)
+        cross = jnp.zeros_like(gram)
+        for k, ref in enumerate((near, far)):
+            whole = ref[...]
+            upper = whole.astype(bf16)
+            lower = (whole - upper.astype(f32)).astype(bf16)
+            turned = upper.astype(f32).T.astype(bf16)
+            flipped[:, half * k : half * (k + 1)] = turned
+            cross += jnp.dot(turned, lower, preferred_element_type=f32)
+            total += lax.dot_general(lower, lower, contract, preferred_element_type=f32)
+            total += jnp.dot(turned, upper, preferred_element_type=f32)
+        gram[...] = total + (cross + cross.T)
 
     product = jnp.dot(flipped[...], tiles[...], preferred_element_type=f32)
     product = (product * usable[...]).astype(bf16)
@@ -202,16 +252,17 @@
         out[k, rank:, :] = own
 
 
-def project(sketch, tiles, usable, row_devices):
+def project(near, far, tiles, usable, row_devices):
     nrows, ncols = tiles.shape
-    rank = sketch.shape[1]
+    half, rank = near.shape
     width = 512
     dests = width // (ncols // row_devices)
     return pl.pallas_call(
         project_kernel,
         grid=(ncols // width,),
         in_specs=[
-            pl.BlockSpec((nrows, rank), lambda j: (0, 0), pipeline_mode=pl.Buffered(1)),
+            pl.BlockSpec((half, rank), lambda j: (0, 0), pipeline_mode=pl.Buffered(1)),
+            pl.BlockSpec((half, rank), lambda j: (0, 0), pipeline_mode=pl.Buffered(1)),
             pl.BlockSpec((nrows, width), lambda j: (0, j)),
             pl.BlockSpec((1, width), lambda j: (0, j)),
         ],
@@ -219,7 +270,7 @@
         out_shape=jax.ShapeDtypeStruct((row_devices, rank + 24, 128), bf16),
         scratch_shapes=[pltpu.VMEM((rank, nrows), bf16), pltpu.VMEM((rank, rank), f32)],
         name="project", compiler_params=pltpu.CompilerParams(vmem_limit_bytes=14 << 20),
-    )(sketch, tiles, usable)
+    )(near, far, tiles, usable)
 
 
 def fold_kernel(parts, product, band):
@@ -293,19 +344,25 @@
     return out
 
 
-def finish_kernel(scale, sketch, product, bands, basis, projected, inverse):
+def finish_kernel(scale, near, far, product, bands, basis, projected, inverse):
     for i, rows in enumerate(inverse_factor(bands)):
         inverse[8 * i : 8 * i + 8, :] = rows
     contract = (((1,), (1,)), ((), ()))
     high, middle, low = thirds(inverse[...] * scale)
-    whole = sketch[...]
-    upper = whole.astype(bf16)
-    lower = (whole - upper.astype(f32)).astype(bf16)
-    total = lax.dot_general(upper, low, contract, preferred_element_type=f32)
-    total += lax.dot_general(lower, middle, contract, preferred_element_type=f32)
-    total += lax.dot_general(lower, high, contract, preferred_element_type=f32)
-    total += lax.dot_general(upper, middle, contract, preferred_element_type=f32)
-    basis[...] = total + lax.dot_general(upper, high, contract, preferred_element_type=f32)
+    count = bands.shape[0]
+    share = near.shape[0] // count
+    for ref, keeper in zip((near, far), halves()):
+        whole = ref[...]
+        upper = whole.astype(bf16)
+        lower = (whole - upper.astype(f32)).astype(bf16)
+        total = lax.dot_general(upper, low, contract, preferred_element_type=f32)
+        total += lax.dot_general(lower, middle, contract, preferred_element_type=f32)
+        total += lax.dot_general(lower, high, contract, preferred_element_type=f32)
+        total += lax.dot_general(upper, middle, contract, preferred_element_type=f32)
+        total += lax.dot_general(upper, high, contract, preferred_element_type=f32)
+        for k in range(count):
+            rows = pl.ds(pl.multiple_of(share * (2 * k + keeper), share), share)
+            basis[rows, :] = total[share * k : share * (k + 1)]
     projected[...] = lax.dot_general(
         product[...].T,
         inverse[...],
@@ -315,34 +372,31 @@
     )
 
 
-def finish(sketch, product, bands, scale):
+def finish(near, far, product, bands, scale):
     return pl.pallas_call(
         functools.partial(finish_kernel, scale),
         out_shape=[
-            jax.ShapeDtypeStruct(sketch.shape, f32),
+            jax.ShapeDtypeStruct((2 * near.shape[0], near.shape[1]), f32),
             jax.ShapeDtypeStruct(product.shape, f32),
         ],
         scratch_shapes=[pltpu.VMEM(product.shape, f32)],
         name="finish", compiler_params=pltpu.CompilerParams(vmem_limit_bytes=8 << 20),
-    )(sketch, product, bands)
+    )(near, far, product, bands)
 
 
 def shards(targets, sources, weights, counts, omega):
     rows_here, cols_here, rank = targets.shape[1], sources.shape[1], omega.shape[1]
     row_devices, col_devices = lax.axis_size("rows"), lax.axis_size("cols")
-    panel_count = counts.shape[0]
-    usable = (
-        (lax.broadcasted_iota(jnp.int32, (panel_count, cols_here // panel_count), 1) < counts[:, None])
-        .reshape(1, cols_here)
-        .astype(f32)
+    tiles, partial, usable = make_sketch(
+        targets, sources, weights.reshape(1, -1), counts.reshape(1, -1), omega, col_devices
     )
-    tiles, partial = make_sketch(targets, sources, weights.reshape(1, cols_here), usable, omega)
-    pieces = lax.all_to_all(partial.reshape(col_devices, -1, rank), "cols", 0, 0)
-    sketch = lax.all_to_all(add_pieces(pieces), "cols", 0, 0).reshape(rows_here, rank)
-    terms = lax.all_to_all(project(sketch, tiles, usable, row_devices), "rows", 0, 0)
+    pieces = lax.all_to_all(partial, "cols", 0, 0)
+    near = lax.all_to_all(add_pieces(pieces), "cols", 0, 0).reshape(rows_here // 2, rank)
+    far = lax.ppermute(near, "cols", [(c, c ^ 1) for c in range(col_devices)])
+    terms = lax.all_to_all(project(near, far, tiles, usable, row_devices), "rows", 0, 0)
     product, band = fold(terms, col_devices)
     bands = lax.all_to_all(band, "cols", 0, 0)
-    return finish(sketch, product, bands, math.sqrt(rows_here * row_devices))
+    return finish(near, far, product, bands, math.sqrt(rows_here * row_devices))
 
 
 def solution(mesh):

time: 163 us -> 152 us (0.933)
  blocking collectives: 114 us -> 103 us
  local copies, waits for them, and re-layouts: 3.64 us -> 0 us
  starting transfers between devices: 0 us -> 1.91 us
  waiting for transfers between devices: 0 us -> 1.88 us
    all_to_all x3, blocking collectives: 102 us -> 90.8 us  [the longest x1 44.3 us: shards(): lax.all_to_all(project(near, far, tiles, usable, row_devices), 'rows', 0, 0)]
    unnamed x8 -> x0, local copies, waits for them, and re-layouts: 3.53 us -> none
    ppermute x0 -> x1, starting transfers between devices: none -> 1.91 us  [shards(): far = lax.ppermute(near, 'cols', [(c, c ^ 1) for c in range(col_devices)])]
    ppermute x0 -> x1, waiting for transfers between devices: none -> 1.88 us  [shards(): far = lax.ppermute(near, 'cols', [(c, c ^ 1) for c in range(col_devices)])]
  transfers between devices with their start and end apart: 0 -> 1, of which waited for: 0 -> 1; matrix products, arithmetic and copies ran while one was open for 0% -> 0% of each run, Pallas kernels for 0% -> 0%
where the time goes in v4:
time: 152 us
  blocking collectives  103 us (68%)
  Pallas kernels  44.2 us (29%)
  starting transfers between devices  1.91 us (1%)
  waiting for transfers between devices  1.88 us (1%)
    all_to_all x1, blocking collectives, shards(): lax.all_to_all(project(near, far, tiles, usable, row_devices), 'rows', 0, 0)  44.3 us
    pallas_call x1, Pallas kernels, make_sketch(): pl.pallas_call(sketch_kernel, grid=(ncols // source_tile,), in_specs=[pl....  30.3 us
    all_to_all x1, blocking collectives, shards(): pieces = lax.all_to_all(partial, 'cols', 0, 0)  26.6 us
    all_to_all x1, blocking collectives, shards(): lax.all_to_all(add_pieces(pieces), 'cols', 0, 0)  19.9 us
    all_to_all x1, blocking collectives, shards(): bands = lax.all_to_all(band, 'cols', 0, 0)  12.1 us
    pallas_call x1, Pallas kernels, finish(): pl.pallas_call(functools.partial(finish_kernel, scale), out_shape=[jax.Sh...  7.98 us
    pallas_call x1, Pallas kernels, project(): pl.pallas_call(project_kernel, grid=(ncols // width,), in_specs=[pl.Block...  5.69 us
  transfers between devices with their start and end apart: 1, of which 1 were waited for; matrix products, arithmetic and copies ran while one was open for 0% of the time, Pallas kernels for 0%

profile of v4, /device:TPU:1, one launch (start us, length us, event | category | flops | bytes accessed | tf_op | source)
XLA Modules:
  0.0 151.6 jit_solution(778931444095777044)
XLA Ops:
  0.6 30.3 %sketch.1 = (bf16[2048,4096]{1,0:T(8,128)(2,1)S(1)}, bf16[16,128,128]{2,1,0:T(8,128)(2,1)S(1)}, f32[1,4096]{1,0:T(1,128)S(1)}) custom-call(f32[3,2048]{1,0:T(4,128)} %targets_in.1, f32[3,4096]{1,0:T(4,128)} %sources_in.1, f32[1,4096]{1,0:T(1,128)} %bitcast.6, s32[1,256]{1,0:T(1,128)} %bitcast.7, bf16[4096,128]{1,0:T(8,128)(2,1)} %omega_in.1), custom_call_target="tpu_custom_call" | custom-call | tf_op jit(solution)/shard_map/sketch/pallas_call | solution.py:169
  30.9 26.6 %all_to_all.20.parts = bf16[16,128,128]{2,1,0:T(8,128)(2,1)S(1)} all-to-all(bf16[16,128,128]{2,1,0:T(8,128)(2,1)S(1)} %get-tuple-element.7), channel_id=1, replica_groups=mesh['rows'=32,'cols'=16] {'cols'}, dimensions={0} | all-to-all | bytes 1048576 | tf_op jit(solution)/shard_map/all_to_all | solution.py:393
  57.5 0.1 pieces.1
  57.6 19.9 %all_to_all.21 = f32[16,64,128]{2,1,0:T(8,128)S(1)} all-to-all(f32[16,64,128]{2,1,0:T(8,128)S(1)} %pieces.1), channel_id=1, replica_groups=mesh['rows'=32,'cols'=16] {'cols'}, dimensions={0} | all-to-all | bytes 1048576 | tf_op jit(solution)/shard_map/all_to_all | solution.py:394
  77.5 1.9 %collective-permute-start = (f32[1024,128]{1,0:T(8,128)S(1)}, f32[1024,128]{1,0:T(8,128)S(1)}, u32[]{:S(2)}, u32[]{:S(2)}) collective-permute-start(f32[1024,128]{1,0:T(8,128)S(1)} %bitcast.3), channel_id=1, source_target_pairs={{0,1},{1,0},{2,3},{3,2},{4,5},{5,4},{6,7},{7,6},{8,9},{9,8},{10,11... | collective-permute-start | bytes 1572872 | tf_op jit(solution)/shard_map/ppermute | solution.py:395
  79.4 1.9 %collective-permute-done.far = f32[1024,128]{1,0:T(8,128)S(1)} collective-permute-done((f32[1024,128]{1,0:T(8,128)S(1)}, f32[1024,128]{1,0:T(8,128)S(1)}, u32[]{:S(2)}, u32[]{:S(2)}) %collective-permute-start) | collective-permute-done | bytes 524320 | tf_op jit(solution)/shard_map/ppermute | solution.py:395
  81.3 5.7 %project.1 = bf16[32,152,128]{2,1,0:T(8,128)(2,1)S(1)} custom-call(f32[1024,128]{1,0:T(8,128)S(1)} %bitcast.4, f32[1024,128]{1,0:T(8,128)S(1)} %collective-permute-done.far, bf16[2048,4096]{1,0:T(8,128)(2,1)S(1)} %get-tuple-element.8.tiles, f32[1,4096]{1,0:T(1,128)S(1)} %get-tuple-element.9.usable), custom_call_target="tpu_custom_call" | custom-call | tf_op jit(solution)/shard_map/project/pallas_call | solution.py:260
  87.0 44.3 %all_to_all.22.parts = bf16[32,152,128]{2,1,0:T(8,128)(2,1)S(1)} all-to-all(bf16[32,152,128]{2,1,0:T(8,128)(2,1)S(1)} %project.1), channel_id=1, replica_groups=mesh['rows'=32,'cols'=16] {'rows'}, dimensions={0} | all-to-all | bytes 2490368 | tf_op jit(solution)/shard_map/all_to_all | solution.py:396
  131.3 0.2 fold.1
  131.5 12.1 %all_to_all.23.bands = f32[16,8,128]{2,1,0:T(8,128)S(1)} all-to-all(f32[16,8,128]{2,1,0:T(8,128)S(1)} %get-tuple-element.11), channel_id=1, replica_groups=mesh['rows'=32,'cols'=16] {'cols'}, dimensions={0} | all-to-all | bytes 131072 | tf_op jit(solution)/shard_map/all_to_all | solution.py:398
  143.6 8.0 %finish.1 = (f32[2048,128]{1,0:T(8,128)}, f32[128,128]{1,0:T(8,128)}) custom-call(f32[1024,128]{1,0:T(8,128)S(1)} %bitcast.5, f32[1024,128]{1,0:T(8,128)S(1)} %collective-permute-done.far, f32[128,128]{1,0:T(8,128)S(1)} %get-tuple-element.10.product, f32[16,8,128]{2,1,0:T(8,128)S(1)} %all_to_all.23.bands), custom_call_target="tpu_custom_call" | custom-call | tf_op jit(solution)/shard_map/finish/pallas_call | solution.py:376
Async XLA Ops:
  77.5 3.8 %collective-permute-start = (f32[1024,128]{1,0:T(8,128)S(1)}, f32[1024,128]{1,0:T(8,128)S(1)}, u32[]{:S(2)}, u32[]{:S(2)}) collective-permute-start(f32[1024,128]{1,0:T(8,128)S(1)} %bitcast.3), channel_id=1, source_target_pairs={{0,1},{1,0},{2,3},{3,2},{4,5},{5,4},{6,7},{7,6},{8,9},{9,8},{10,11... | collective-permute-start | bytes 1572872 | tf_op jit(solution)/shard_map/ppermute | solution.py:395

commit v5 on v4

--- a/solution.py
+++ b/solution.py
@@ -14,7 +14,7 @@
 separation = 2.0
 turns = wave_number / (2.0 * math.pi)
 sine = (6.283164043875678, -41.33714231633244, 81.34076713243772, -70.99341720807224)
-target_tile = 512
+target_tile = 1024
 source_tile = 512
 
 
@@ -48,7 +48,7 @@
 
 
 def sketch_kernel(targets_in, sources_in, weights_in, counts_in, omega_in, tiles, sketch, usable,
-                  targets, sources, weights, counts, omega, arrived, feature, tfeat, afeat, bfeat, masked, a_even, b_even, k_even, a_odd, b_odd, k_odd, acc):
+                  targets, sources, weights, counts, omega, arrived, feature, tfeat, afeat, bfeat, masked, k_even, k_odd, acc):
     step = pl.program_id(0)
     nrows, ncols = targets.shape[1], sources.shape[1]
     per_step = nrows // target_tile
@@ -56,25 +56,6 @@
 
     def block(at, size):
         return pl.ds(pl.multiple_of(at * size, size), size)
-
-    def distances(tile, a_buf, b_buf):
-        here = tfeat[block(lax.rem(tile, per_step), target_tile), :]
-        there = block(lax.div(tile, per_step), source_tile)
-        a_buf[...] = jnp.dot(here, afeat[:, there], preferred_element_type=f32)
-        b_buf[...] = jnp.dot(here, bfeat[:, there], preferred_element_type=f32)
-
-    def evaluate(tile, a_buf, b_buf, k_buf):
-        first = lax.rem(tile, per_step) * target_tile
-        for r in range(0, target_tile, 16):
-            over = lax.rsqrt(a_buf[r : r + 16, :])
-            turn = b_buf[r : r + 16, :] * over
-            away = 0.25 - jnp.abs(turn - jnp.round(turn))
-            square = away * away
-            c0, c1, c2, c3 = (turns * c for c in sine)
-            wave = ((c3 * square + c2) * square + c1) * square + c0
-            low = ((wave * away) * over).astype(bf16)
-            k_buf[r : r + 16, :] = low
-            tiles[pl.ds(pl.multiple_of(first + r, 16), 16), :] = low
 
     def accumulate(tile, k_buf):
         rows = block(lax.rem(tile, per_step), target_tile)
@@ -114,7 +95,7 @@
         sy = (sources[1:2, :] - 0.5) * turns
         sz = (sources[2:3, :] - 0.5) * turns
         norm = sx * sx + sy * sy + sz * sz
-        inverse = 1.0 / weights[...]
+        inverse = (1.0 / (-sine[3] * turns)) / weights[...]
         for ref, scale in ((bfeat, inverse), (afeat, inverse * inverse)):
             rows = [-2.0 * sx * scale, -2.0 * sy * scale, -2.0 * sz * scale, scale, norm * scale]
             put_thirds(feature, pick_rows(rows, (8, ncols)), False)
@@ -133,7 +114,6 @@
         for k in range(ncols // 128):
             usable[0:1, 128 * k : 128 * k + 128] = flags[k : k + 1, :]
         moves[4].wait()
-        distances(0, a_even, b_even)
         columns = flags.T
         for k in range(ncols // 128):
             rows = slice(128 * k, 128 * k + 128)
@@ -143,13 +123,20 @@
         k_odd[...] = jnp.zeros_like(k_odd)
 
     def pair(p, carry):
-        tile = step * per_step + 2 * p
-        distances(tile + 1, a_odd, b_odd)
-        evaluate(tile, a_even, b_even, k_even)
-        accumulate(jnp.maximum(tile - 1, 0), k_odd)
-        distances(jnp.minimum(tile + 2, total - 1), a_even, b_even)
-        evaluate(tile + 1, a_odd, b_odd, k_odd)
-        accumulate(tile, k_even)
+        for odd, (k_now, k_last) in enumerate(((k_even, k_odd), (k_odd, k_even))):
+            tile = step * per_step + 2 * p + odd
+            there = block(lax.div(tile, per_step), source_tile)
+            for part in range(target_tile // 256):
+                at = block(lax.rem(tile, per_step) * (target_tile // 256) + part, 256)
+                over = lax.rsqrt(jnp.dot(tfeat[at, :], afeat[:, there], preferred_element_type=f32))
+                turn = jnp.dot(tfeat[at, :], bfeat[:, there], preferred_element_type=f32) * over
+                away = jnp.abs(turn - jnp.round(turn)) - 0.25
+                square = away * away
+                wave = ((square + sine[2] / sine[3]) * square + sine[1] / sine[3]) * square + sine[0] / sine[3]
+                low = ((wave * away) * over).astype(bf16)
+                k_now[256 * part : 256 * (part + 1), :] = low
+                tiles[at, :] = low
+            accumulate(jnp.maximum(tile - 1, 0), k_last)
         return carry
 
     lax.fori_loop(0, per_step // 2, pair, 0)
@@ -192,11 +179,7 @@
             pltpu.VMEM((128, ncols), bf16),
             pltpu.VMEM((128, ncols), bf16),
             pltpu.VMEM((ncols, rank), bf16),
-            pltpu.VMEM((target_tile, source_tile), f32),
-            pltpu.VMEM((target_tile, source_tile), f32),
             pltpu.VMEM((target_tile, source_tile), bf16),
-            pltpu.VMEM((target_tile, source_tile), f32),
-            pltpu.VMEM((target_tile, source_tile), f32),
             pltpu.VMEM((target_tile, source_tile), bf16),
             pltpu.VMEM((nrows, rank), f32),
         ],
@@ -245,7 +228,7 @@
     product = jnp.dot(flipped[...], tiles[...], preferred_element_type=f32)
     product = (product * usable[...]).astype(bf16)
     first = pl.multiple_of(lax.axis_index("cols") * band, band)
-    own = jnp.concatenate([part.astype(f32) for part in thirds(gram[pl.ds(first, band), :])], axis=0)
+    own = jnp.concatenate([part.astype(f32) for part in thirds(gram[pl.ds(first, band), :])[0:2]], axis=0)
     own = own.astype(bf16)
     for k in range(out.shape[0]):
         out[k, 0:rank, :] = product[:, 128 * k : 128 * k + 128]
@@ -266,8 +249,8 @@
             pl.BlockSpec((nrows, width), lambda j: (0, j)),
             pl.BlockSpec((1, width), lambda j: (0, j)),
         ],
-        out_specs=pl.BlockSpec((dests, rank + 24, 128), lambda j: (j, 0, 0)),
-        out_shape=jax.ShapeDtypeStruct((row_devices, rank + 24, 128), bf16),
+        out_specs=pl.BlockSpec((dests, rank + 16, 128), lambda j: (j, 0, 0)),
+        out_shape=jax.ShapeDtypeStruct((row_devices, rank + 16, 128), bf16),
         scratch_shapes=[pltpu.VMEM((rank, nrows), bf16), pltpu.VMEM((rank, rank), f32)],
         name="project", compiler_params=pltpu.CompilerParams(vmem_limit_bytes=14 << 20),
     )(near, far, tiles, usable)
@@ -280,15 +263,13 @@
     rank = product.shape[0]
     rows = band.shape[1]
     product[...] = total[0:rank]
-    own = total[rank : rank + rows] + (
-        total[rank + rows : rank + 2 * rows] + total[rank + 2 * rows : rank + 3 * rows]
-    )
+    own = total[rank : rank + rows] + total[rank + rows : rank + 2 * rows]
     for k in range(band.shape[0]):
         band[k] = own
 
 
 def fold(parts, col_devices):
-    rank = parts.shape[1] - 24
+    rank = parts.shape[1] - 16
     return pl.pallas_call(
         fold_kernel,
         out_shape=[
@@ -344,11 +325,19 @@
     return out
 
 
-def finish_kernel(scale, near, far, product, bands, basis, projected, inverse):
+def finish_kernel(scale, near_in, far_in, product, bands, basis, projected, inverse, near, far, arrived):
+    moves = [
+        pltpu.make_async_copy(near_in, near, arrived.at[0]),
+        pltpu.make_async_copy(far_in, far, arrived.at[1]),
+    ]
+    for move in moves:
+        move.start()
     for i, rows in enumerate(inverse_factor(bands)):
         inverse[8 * i : 8 * i + 8, :] = rows
     contract = (((1,), (1,)), ((), ()))
     high, middle, low = thirds(inverse[...] * scale)
+    for move in moves:
+        move.wait()
     count = bands.shape[0]
     share = near.shape[0] // count
     for ref, keeper in zip((near, far), halves()):
@@ -379,7 +368,18 @@
             jax.ShapeDtypeStruct((2 * near.shape[0], near.shape[1]), f32),
             jax.ShapeDtypeStruct(product.shape, f32),
         ],
-        scratch_shapes=[pltpu.VMEM(product.shape, f32)],
+        in_specs=[
+            pl.BlockSpec(memory_space=pl.ANY),
+            pl.BlockSpec(memory_space=pl.ANY),
+            pl.BlockSpec(memory_space=pltpu.VMEM),
+            pl.BlockSpec(memory_space=pltpu.VMEM),
+        ],
+        scratch_shapes=[
+            pltpu.VMEM(product.shape, f32),
+            pltpu.VMEM(near.shape, f32),
+            pltpu.VMEM(far.shape, f32),
+            pltpu.SemaphoreType.DMA((2,)),
+        ],
         name="finish", compiler_params=pltpu.CompilerParams(vmem_limit_bytes=8 << 20),
     )(near, far, product, bands)
 

time: 152 us -> 148 us (0.974)
  Pallas kernels: 44.2 us -> 41 us
    pallas_call x1, Pallas kernels: 30.3 us -> 26.9 us  [make_sketch(): pl.pallas_call(sketch_kernel, grid=(ncols // source_tile,), in_specs=[pl....]
where the time goes in v5:
time: 148 us
  blocking collectives  102 us (69%)
  Pallas kernels  41 us (28%)
  starting transfers between devices  1.91 us (1%)
  waiting for transfers between devices  1.88 us (1%)
    all_to_all x1, blocking collectives, shards(): lax.all_to_all(project(near, far, tiles, usable, row_devices), 'rows', 0, 0)  43.8 us
    pallas_call x1, Pallas kernels, make_sketch(): pl.pallas_call(sketch_kernel, grid=(ncols // source_tile,), in_specs=[pl....  26.9 us
    all_to_all x1, blocking collectives, shards(): pieces = lax.all_to_all(partial, 'cols', 0, 0)  26.6 us
    all_to_all x1, blocking collectives, shards(): lax.all_to_all(add_pieces(pieces), 'cols', 0, 0)  19.9 us
    all_to_all x1, blocking collectives, shards(): bands = lax.all_to_all(band, 'cols', 0, 0)  12 us
    pallas_call x1, Pallas kernels, finish(): pl.pallas_call(functools.partial(finish_kernel, scale), out_shape=[jax.Sh...  8.1 us
    pallas_call x1, Pallas kernels, project(): pl.pallas_call(project_kernel, grid=(ncols // width,), in_specs=[pl.Block...  5.69 us
  transfers between devices with their start and end apart: 1, of which 1 were waited for; matrix products, arithmetic and copies ran while one was open for 0% of the time, Pallas kernels for 0%

profile of v5, /device:TPU:1, one launch (start us, length us, event | category | flops | bytes accessed | tf_op | source)
XLA Modules:
  0.0 147.8 jit_solution(17953366765571783331)
XLA Ops:
  0.6 26.9 %sketch.1 = (bf16[2048,4096]{1,0:T(8,128)(2,1)S(1)}, bf16[16,128,128]{2,1,0:T(8,128)(2,1)S(1)}, f32[1,4096]{1,0:T(1,128)S(1)}) custom-call(f32[3,2048]{1,0:T(4,128)} %targets_in.1, f32[3,4096]{1,0:T(4,128)} %sources_in.1, f32[1,4096]{1,0:T(1,128)} %bitcast.6, s32[1,256]{1,0:T(1,128)} %bitcast.7, bf16[4096,128]{1,0:T(8,128)(2,1)} %omega_in.1), custom_call_target="tpu_custom_call" | custom-call | tf_op jit(solution)/shard_map/sketch/pallas_call | solution.py:156
  27.6 26.6 %all_to_all.20.parts = bf16[16,128,128]{2,1,0:T(8,128)(2,1)S(1)} all-to-all(bf16[16,128,128]{2,1,0:T(8,128)(2,1)S(1)} %get-tuple-element.7), channel_id=1, replica_groups=mesh['rows'=32,'cols'=16] {'cols'}, dimensions={0} | all-to-all | bytes 1048576 | tf_op jit(solution)/shard_map/all_to_all | solution.py:393
  54.2 0.1 pieces.1
  54.2 19.9 %all_to_all.21 = f32[16,64,128]{2,1,0:T(8,128)S(1)} all-to-all(f32[16,64,128]{2,1,0:T(8,128)S(1)} %pieces.1), channel_id=1, replica_groups=mesh['rows'=32,'cols'=16] {'cols'}, dimensions={0} | all-to-all | bytes 1048576 | tf_op jit(solution)/shard_map/all_to_all | solution.py:394
  74.2 1.9 %collective-permute-start = (f32[1024,128]{1,0:T(8,128)S(1)}, f32[1024,128]{1,0:T(8,128)S(1)}, u32[]{:S(2)}, u32[]{:S(2)}) collective-permute-start(f32[1024,128]{1,0:T(8,128)S(1)} %bitcast.3), channel_id=1, source_target_pairs={{0,1},{1,0},{2,3},{3,2},{4,5},{5,4},{6,7},{7,6},{8,9},{9,8},{10,11... | collective-permute-start | bytes 1572872 | tf_op jit(solution)/shard_map/ppermute | solution.py:395
  76.1 1.9 %collective-permute-done.far.far_in = f32[1024,128]{1,0:T(8,128)S(1)} collective-permute-done((f32[1024,128]{1,0:T(8,128)S(1)}, f32[1024,128]{1,0:T(8,128)S(1)}, u32[]{:S(2)}, u32[]{:S(2)}) %collective-permute-start) | collective-permute-done | bytes 524320 | tf_op jit(solution)/shard_map/ppermute | solution.py:395
  78.0 5.7 %project.1 = bf16[32,144,128]{2,1,0:T(8,128)(2,1)S(1)} custom-call(f32[1024,128]{1,0:T(8,128)S(1)} %bitcast.4, f32[1024,128]{1,0:T(8,128)S(1)} %collective-permute-done.far.far_in, bf16[2048,4096]{1,0:T(8,128)(2,1)S(1)} %get-tuple-element.8.tiles, f32[1,4096]{1,0:T(1,128)S(1)} %get-tuple-element.9.usable), custom_call_target="tpu_custom_call" | custom-call | tf_op jit(solution)/shard_map/project/pallas_call | solution.py:243
  83.7 43.8 %all_to_all.22.parts = bf16[32,144,128]{2,1,0:T(8,128)(2,1)S(1)} all-to-all(bf16[32,144,128]{2,1,0:T(8,128)(2,1)S(1)} %project.1), channel_id=1, replica_groups=mesh['rows'=32,'cols'=16] {'rows'}, dimensions={0} | all-to-all | bytes 2359296 | tf_op jit(solution)/shard_map/all_to_all | solution.py:396
  127.5 0.2 fold.1
  127.6 12.0 %all_to_all.23.bands = f32[16,8,128]{2,1,0:T(8,128)S(1)} all-to-all(f32[16,8,128]{2,1,0:T(8,128)S(1)} %get-tuple-element.11), channel_id=1, replica_groups=mesh['rows'=32,'cols'=16] {'cols'}, dimensions={0} | all-to-all | bytes 131072 | tf_op jit(solution)/shard_map/all_to_all | solution.py:398
  139.7 8.1 %finish.1 = (f32[2048,128]{1,0:T(8,128)}, f32[128,128]{1,0:T(8,128)}) custom-call(f32[1024,128]{1,0:T(8,128)S(1)} %bitcast.5, f32[1024,128]{1,0:T(8,128)S(1)} %collective-permute-done.far.far_in, f32[128,128]{1,0:T(8,128)S(1)} %get-tuple-element.10.product, f32[16,8,128]{2,1,0:T(8,128)S(1)} %all_to_all.23.bands), custom_call_target="tpu_custom_call" | custom-call | tf_op jit(solution)/shard_map/finish/pallas_call | solution.py:365
Async XLA Ops:
  74.2 3.8 %collective-permute-start = (f32[1024,128]{1,0:T(8,128)S(1)}, f32[1024,128]{1,0:T(8,128)S(1)}, u32[]{:S(2)}, u32[]{:S(2)}) collective-permute-start(f32[1024,128]{1,0:T(8,128)S(1)} %bitcast.3), channel_id=1, source_target_pairs={{0,1},{1,0},{2,3},{3,2},{4,5},{5,4},{6,7},{7,6},{8,9},{9,8},{10,11... | collective-permute-start | bytes 1572872 | tf_op jit(solution)/shard_map/ppermute | solution.py:395

commit v6 on v5

--- a/solution.py
+++ b/solution.py
@@ -77,7 +77,7 @@
         ]
         for move in moves:
             move.start()
-        feature[...] = jnp.zeros_like(feature)
+        feature[72:80, :] = jnp.zeros((8, ncols), f32)
         moves[0].wait()
         tx = (targets[0:1, :] - (0.5 + 0.5 * separation)) * turns
         ty = (targets[1:2, :] - 0.5) * turns
@@ -174,10 +174,10 @@
             pltpu.VMEM(counts.shape, jnp.int32),
             pltpu.VMEM((ncols, rank), bf16),
             pltpu.SemaphoreType.DMA((5,)),
-            pltpu.VMEM((128, ncols), f32),
-            pltpu.VMEM((nrows, 128), bf16),
-            pltpu.VMEM((128, ncols), bf16),
-            pltpu.VMEM((128, ncols), bf16),
+            pltpu.VMEM((80, ncols), f32),
+            pltpu.VMEM((nrows, 80), bf16),
+            pltpu.VMEM((80, ncols), bf16),
+            pltpu.VMEM((80, ncols), bf16),
             pltpu.VMEM((ncols, rank), bf16),
             pltpu.VMEM((target_tile, source_tile), bf16),
             pltpu.VMEM((target_tile, source_tile), bf16),

time: 148 us -> 147 us (level)
  no operation moved by 1% of the time
where the time goes in v6:
time: 147 us
  blocking collectives  102 us (69%)
  Pallas kernels  40.3 us (27%)
  starting transfers between devices  1.91 us (1%)
  waiting for transfers between devices  1.88 us (1%)
    all_to_all x1, blocking collectives, shards(): lax.all_to_all(project(near, far, tiles, usable, row_devices), 'rows', 0, 0)  43.8 us
    all_to_all x1, blocking collectives, shards(): pieces = lax.all_to_all(partial, 'cols', 0, 0)  26.6 us
    pallas_call x1, Pallas kernels, make_sketch(): pl.pallas_call(sketch_kernel, grid=(ncols // source_tile,), in_specs=[pl....  26.2 us
    all_to_all x1, blocking collectives, shards(): lax.all_to_all(add_pieces(pieces), 'cols', 0, 0)  19.9 us
    all_to_all x1, blocking collectives, shards(): bands = lax.all_to_all(band, 'cols', 0, 0)  12 us
    pallas_call x1, Pallas kernels, finish(): pl.pallas_call(functools.partial(finish_kernel, scale), out_shape=[jax.Sh...  8.1 us
    pallas_call x1, Pallas kernels, project(): pl.pallas_call(project_kernel, grid=(ncols // width,), in_specs=[pl.Block...  5.69 us
  transfers between devices with their start and end apart: 1, of which 1 were waited for; matrix products, arithmetic and copies ran while one was open for 0% of the time, Pallas kernels for 0%

profile of v6, /device:TPU:1, one launch (start us, length us, event | category | flops | bytes accessed | tf_op | source)
XLA Modules:
  0.0 147.1 jit_solution(17872173716763464058)
XLA Ops:
  0.6 26.2 %sketch.1 = (bf16[2048,4096]{1,0:T(8,128)(2,1)S(1)}, bf16[16,128,128]{2,1,0:T(8,128)(2,1)S(1)}, f32[1,4096]{1,0:T(1,128)S(1)}) custom-call(f32[3,2048]{1,0:T(4,128)} %targets_in.1, f32[3,4096]{1,0:T(4,128)} %sources_in.1, f32[1,4096]{1,0:T(1,128)} %bitcast.6, s32[1,256]{1,0:T(1,128)} %bitcast.7, bf16[4096,128]{1,0:T(8,128)(2,1)} %omega_in.1), custom_call_target="tpu_custom_call" | custom-call | tf_op jit(solution)/shard_map/sketch/pallas_call | solution.py:156
  26.9 26.6 %all_to_all.20.parts = bf16[16,128,128]{2,1,0:T(8,128)(2,1)S(1)} all-to-all(bf16[16,128,128]{2,1,0:T(8,128)(2,1)S(1)} %get-tuple-element.7), channel_id=1, replica_groups=mesh['rows'=32,'cols'=16] {'cols'}, dimensions={0} | all-to-all | bytes 1048576 | tf_op jit(solution)/shard_map/all_to_all | solution.py:393
  53.4 0.1 pieces.1
  53.5 19.9 %all_to_all.21 = f32[16,64,128]{2,1,0:T(8,128)S(1)} all-to-all(f32[16,64,128]{2,1,0:T(8,128)S(1)} %pieces.1), channel_id=1, replica_groups=mesh['rows'=32,'cols'=16] {'cols'}, dimensions={0} | all-to-all | bytes 1048576 | tf_op jit(solution)/shard_map/all_to_all | solution.py:394
  73.4 1.9 %collective-permute-start = (f32[1024,128]{1,0:T(8,128)S(1)}, f32[1024,128]{1,0:T(8,128)S(1)}, u32[]{:S(2)}, u32[]{:S(2)}) collective-permute-start(f32[1024,128]{1,0:T(8,128)S(1)} %bitcast.3), channel_id=1, source_target_pairs={{0,1},{1,0},{2,3},{3,2},{4,5},{5,4},{6,7},{7,6},{8,9},{9,8},{10,11... | collective-permute-start | bytes 1572872 | tf_op jit(solution)/shard_map/ppermute | solution.py:395
  75.4 1.9 %collective-permute-done.far.far_in = f32[1024,128]{1,0:T(8,128)S(1)} collective-permute-done((f32[1024,128]{1,0:T(8,128)S(1)}, f32[1024,128]{1,0:T(8,128)S(1)}, u32[]{:S(2)}, u32[]{:S(2)}) %collective-permute-start) | collective-permute-done | bytes 524320 | tf_op jit(solution)/shard_map/ppermute | solution.py:395
  77.2 5.7 %project.1 = bf16[32,144,128]{2,1,0:T(8,128)(2,1)S(1)} custom-call(f32[1024,128]{1,0:T(8,128)S(1)} %bitcast.4, f32[1024,128]{1,0:T(8,128)S(1)} %collective-permute-done.far.far_in, bf16[2048,4096]{1,0:T(8,128)(2,1)S(1)} %get-tuple-element.8.tiles, f32[1,4096]{1,0:T(1,128)S(1)} %get-tuple-element.9.usable), custom_call_target="tpu_custom_call" | custom-call | tf_op jit(solution)/shard_map/project/pallas_call | solution.py:243
  82.9 43.8 %all_to_all.22.parts = bf16[32,144,128]{2,1,0:T(8,128)(2,1)S(1)} all-to-all(bf16[32,144,128]{2,1,0:T(8,128)(2,1)S(1)} %project.1), channel_id=1, replica_groups=mesh['rows'=32,'cols'=16] {'rows'}, dimensions={0} | all-to-all | bytes 2359296 | tf_op jit(solution)/shard_map/all_to_all | solution.py:396
  126.8 0.2 fold.1
  126.9 12.0 %all_to_all.23.bands = f32[16,8,128]{2,1,0:T(8,128)S(1)} all-to-all(f32[16,8,128]{2,1,0:T(8,128)S(1)} %get-tuple-element.11), channel_id=1, replica_groups=mesh['rows'=32,'cols'=16] {'cols'}, dimensions={0} | all-to-all | bytes 131072 | tf_op jit(solution)/shard_map/all_to_all | solution.py:398
  139.0 8.1 %finish.1 = (f32[2048,128]{1,0:T(8,128)}, f32[128,128]{1,0:T(8,128)}) custom-call(f32[1024,128]{1,0:T(8,128)S(1)} %bitcast.5, f32[1024,128]{1,0:T(8,128)S(1)} %collective-permute-done.far.far_in, f32[128,128]{1,0:T(8,128)S(1)} %get-tuple-element.10.product, f32[16,8,128]{2,1,0:T(8,128)S(1)} %all_to_all.23.bands), custom_call_target="tpu_custom_call" | custom-call | tf_op jit(solution)/shard_map/finish/pallas_call | solution.py:365
Async XLA Ops:
  73.4 3.8 %collective-permute-start = (f32[1024,128]{1,0:T(8,128)S(1)}, f32[1024,128]{1,0:T(8,128)S(1)}, u32[]{:S(2)}, u32[]{:S(2)}) collective-permute-start(f32[1024,128]{1,0:T(8,128)S(1)} %bitcast.3), channel_id=1, source_target_pairs={{0,1},{1,0},{2,3},{3,2},{4,5},{5,4},{6,7},{7,6},{8,9},{9,8},{10,11... | collective-permute-start | bytes 1572872 | tf_op jit(solution)/shard_map/ppermute | solution.py:395
